TPU v7x, 512 devices: a whole 4x4x16 slice. The times are simulated.
512 devices in a mesh: slab: 128 (over x, z, y_hi), col: 4 (over y_lo, core).
Axes of the slice: x: 4, y: 4 (y_hi: 2, y_lo: 2; y = y_hi * 2 + y_lo), z: 16, core: 2. Of those that a mesh axis runs over, the one named last changes fastest.
Arguments:
- rhs: float32 [1024, 32, 384], P(('slab', 'col')), may hold values from -6 to 6
- tiles: bfloat16 [1024, 6, 384, 384], P(('slab', 'col'))
- neighbours: int32 [1024, 6], P(('slab', 'col')), may hold values from 0 to 1023, as said below
- smoother: bfloat16 [1024, 384, 384], P(('slab', 'col'))
- basis: bfloat16 [1024, 256, 384], P(('slab', 'col')), may hold values from -0.29882812 to 0.29882812
Outputs:
- solution: float32 [1024, 32, 384], P(('slab', 'col'))
- coarse_iterate: float32 [1024, 32, 256], P(('slab', 'col'))
Inputs may be any that keep to these rules, and one draw needn't show every extreme that they name: `neighbours`: entry [g, 0] is g itself; every other entry names a cell whose slab (cell // 8) is the slab of g or one of the two beside it, counted around 128 slabs.
All inputs are finite; a program needn't handle non-finite values.
Results may differ from a plain program's by a relative error of at most 0.0023.
The roundings to bfloat16 on the way count: a program that leaves them out, or rounds other values in their place, can miss the bound.
Values may be sent and summed in bfloat16 or wider, within the bound.
No kernel may reach another device: no remote copies, remote signals or barrier semaphores. Data moves between devices by JAX's collectives and lax.ppermute only.
A program may use at most 128 MiB of HBM per device.

v0:
```python
import jax
import jax.numpy as jnp
from jax import lax
from jax.sharding import PartitionSpec as P

damping = 0.8


def with_halo(cells, sides, width):
    for axis, dim in sides:
        count = lax.axis_size(axis)
        head = lax.slice_in_dim(cells, 0, width, axis=dim)
        tail = lax.slice_in_dim(cells, cells.shape[dim] - width, cells.shape[dim], axis=dim)
        cells = jnp.concatenate(
            [
                lax.ppermute(tail, axis, [(i, (i + 1) % count) for i in range(count)]),
                cells,
                lax.ppermute(head, axis, [((i + 1) % count, i) for i in range(count)]),
            ],
            axis=dim,
        )
    return cells


def neighbour_rows(vec_rounded):
    slab_rows = lax.all_gather(vec_rounded, "col", axis=0, tiled=True)
    return with_halo(slab_rows, (("slab", 0),), slab_rows.shape[0])


def per_device(rhs, tiles, neighbours, smoother, basis):
    cell_dev = rhs.shape[0]
    slab_count = lax.axis_size("slab")
    slab_cells = cell_dev * lax.axis_size("col")
    here = lax.axis_index("slab")
    slab_step = (neighbours // slab_cells - here + 1 + slab_count) % slab_count
    offset = neighbours % slab_cells
    row_place = slab_step * slab_cells + offset

    def smooth(residue):
        return jnp.einsum(
            "gri,gio->gro",
            residue.astype(jnp.bfloat16),
            smoother,
            preferred_element_type=jnp.float32,
        )

    def fine_apply(vec):
        near = neighbour_rows(vec.astype(jnp.bfloat16))
        picked = jnp.take(near, row_place, axis=0)
        return jnp.einsum("gtri,gtio->gro", picked, tiles, preferred_element_type=jnp.float32)

    x_first = smooth(rhs)
    x_second = x_first + smooth(rhs - fine_apply(x_first))
    fine_residual = rhs - fine_apply(x_second)
    wide_basis = lax.all_gather(basis, "col", axis=0, tiled=True)
    near_basis = with_halo(wide_basis, (("slab", 0),), wide_basis.shape[0])
    picked_basis = jnp.take(near_basis, row_place, axis=0)
    upper = jnp.einsum(
        "gtci,gtio->gtco", picked_basis, tiles, preferred_element_type=jnp.float32
    ).astype(jnp.bfloat16)
    coarse_tiles = jnp.einsum(
        "gtco,gdo->gtcd", upper, basis, preferred_element_type=jnp.float32
    ).astype(jnp.bfloat16)
    pivots = jnp.diagonal(coarse_tiles[:, 0].astype(jnp.float32), axis1=1, axis2=2)
    coarse_rhs = jnp.einsum(
        "gri,gci->grc",
        fine_residual.astype(jnp.bfloat16),
        basis,
        preferred_element_type=jnp.float32,
    )
    c_first = damping * coarse_rhs / pivots[:, None, :]
    near_coarse = neighbour_rows(c_first.astype(jnp.bfloat16))
    picked_coarse = jnp.take(near_coarse, row_place, axis=0)
    coarse_image = jnp.einsum(
        "gtrc,gtcd->grd", picked_coarse, coarse_tiles, preferred_element_type=jnp.float32
    )
    coarse_iterate = c_first + damping * (coarse_rhs - coarse_image) / pivots[:, None, :]
    solution = x_second + jnp.einsum(
        "grc,gci->gri",
        coarse_iterate.astype(jnp.bfloat16),
        basis,
        preferred_element_type=jnp.float32,
    )
    return (solution, coarse_iterate)


def solution(mesh):
    placed = (
        P(("slab", "col"), None, None),
        P(("slab", "col"), None, None, None),
        P(("slab", "col"), None),
        P(("slab", "col"), None, None),
        P(("slab", "col"), None, None),
    )
    return jax.shard_map(
        per_device,
        mesh=mesh,
        in_specs=placed,
        out_specs=(P(("slab", "col"), None, None), P(("slab", "col"), None, None)),
        check_vma=False,
    )
```

profile of v0, /device:TPU:1, one launch (start us, length us, event | category | flops | bytes accessed | tf_op | source)
XLA Modules:
  0.0 257.2 jit_solution(5884026762105295184)
XLA Ops:
  7.9 40.4 %all-gather.2.cloned.1.call-done = bf16[8,256,384]{2,1,0:T(8,128)(2,1)} async-done(((bf16[2,256,384]{2,1,0:T(8,128)(2,1)}), bf16[8,256,384]{2,1,0:T(8,128)(2,1)}) %all-gather.2.cloned.1.call-update) | async-done | bytes 1572880 | tf_op jit(solution)/shard_map/all_gather | solution.py:55
  48.3 9.9 %collective-permute-start.5 = (bf16[8,256,384]{2,1,0:T(8,128)(2,1)}, bf16[8,256,384]{2,1,0:T(8,128)(2,1)}, u32[]{:S(2)}, u32[]{:S(2)}) collective-permute-start(bf16[8,256,384]{2,1,0:T(8,128)(2,1)} %all-gather.2.cloned.1.call-done), channel_id=1, source_target_pairs={{4,0},{8,4},{12,8},{16,12},{20,16},{24,20},{28,24},{32,28},{36,32}... | collective-permute-start | bytes 4718600 | tf_op jit(solution)/shard_map/ppermute | solution.py:18
  62.1 62.8 %all_gather.12 = bf16[8,32,384]{2,1,0:T(8,128)(2,1)} all-gather(bf16[2,32,384]{2,1,0:T(8,128)(2,1)S(1)} %get-tuple-element.5), channel_id=1, replica_groups=mesh['slab'=128,'col'=4] {'col'}, dimensions={0}, use_global_device_ids=true | all-gather | bytes 245760 | tf_op jit(solution)/shard_map/all_gather | solution.py:26
  124.9 8.1 %collective-permute-start.1 = (bf16[8,32,384]{2,1,0:T(8,128)(2,1)}, bf16[8,32,384]{2,1,0:T(8,128)(2,1)}, u32[]{:S(2)}, u32[]{:S(2)}) collective-permute-start(bf16[8,32,384]{2,1,0:T(8,128)(2,1)} %all_gather.12), channel_id=1, source_target_pairs={{4,0},{8,4},{12,8},{16,12},{20,16},{24,20},{28,24},{32,28},{36,32}... | collective-permute-start | bytes 589832 | tf_op jit(solution)/shard_map/ppermute | solution.py:18
  137.3 9.6 %collective-permute-done = bf16[8,32,384]{2,1,0:T(8,128)(2,1)} collective-permute-done((bf16[8,32,384]{2,1,0:T(8,128)(2,1)}, bf16[8,32,384]{2,1,0:T(8,128)(2,1)}, u32[]{:S(2)}, u32[]{:S(2)}) %collective-permute-start) | collective-permute-done | bytes 196640 | tf_op jit(solution)/shard_map/ppermute | solution.py:16
  148.9 2.4 gather_fusion.3
  151.3 2.7 %fusion.57 = (bf16[2,32,384]{2,1,0:T(8,128)(2,1)}, f32[2,32,384]{2,1,0:T(8,128)}) fusion(f32[2,32,384]{2,1,0:T(8,128)} %get-tuple-element.6, bf16[2,384,384]{2,1,0:T(8,128)(2,1)} %param.10, f32[2,32,384]{2,1,0:T(8,128)} %param.7, bf16[2,6,384,384]{3,2,1,0:T(8,128)(2,1)S(1)} %copy-done, bf16[2,6,32,384]{3,2,1,0:T(8,128)(2,1)} %bitcast.60, ...), kind=kOutput, calls=%fused_computation.67 | convolution fusion | flops 132366336 | bytes 4767756 | tf_op jit(solution)/shard_map/gri,gio->gro/dot_general | solution.py:40
  154.0 6.9 %all_gather.13 = bf16[8,32,384]{2,1,0:T(8,128)(2,1)S(1)} all-gather(bf16[2,32,384]{2,1,0:T(8,128)(2,1)} %get-tuple-element.7), channel_id=1, replica_groups=mesh['slab'=128,'col'=4] {'col'}, dimensions={0}, use_global_device_ids=true | all-gather | bytes 245760 | tf_op jit(solution)/shard_map/all_gather | solution.py:26
  160.9 4.2 %collective-permute-start.3 = (bf16[8,32,384]{2,1,0:T(8,128)(2,1)S(1)}, bf16[8,32,384]{2,1,0:T(8,128)(2,1)S(1)}, u32[]{:S(2)}, u32[]{:S(2)}) collective-permute-start(bf16[8,32,384]{2,1,0:T(8,128)(2,1)S(1)} %all_gather.13), channel_id=1, source_target_pairs={{4,0},{8,4},{12,8},{16,12},{20,16},{24,20},{28,24},{32,28},{36,32}... | collective-permute-start | bytes 589832 | tf_op jit(solution)/shard_map/ppermute | solution.py:18
  165.1 2.6 %collective-permute-start.2 = (bf16[8,32,384]{2,1,0:T(8,128)(2,1)S(1)}, bf16[8,32,384]{2,1,0:T(8,128)(2,1)S(1)}, u32[]{:S(2)}, u32[]{:S(2)}) collective-permute-start(bf16[8,32,384]{2,1,0:T(8,128)(2,1)S(1)} %all_gather.13), channel_id=1, source_target_pairs={{0,4},{4,8},{8,12},{12,16},{16,20},{20,24},{24,28},{28,32},{32,36}... | collective-permute-start | bytes 589832 | tf_op jit(solution)/shard_map/ppermute | solution.py:16
  167.7 2.9 %collective-permute-done.3 = bf16[8,32,384]{2,1,0:T(8,128)(2,1)S(1)} collective-permute-done((bf16[8,32,384]{2,1,0:T(8,128)(2,1)S(1)}, bf16[8,32,384]{2,1,0:T(8,128)(2,1)S(1)}, u32[]{:S(2)}, u32[]{:S(2)}) %collective-permute-start.3) | collective-permute-done | bytes 196640 | tf_op jit(solution)/shard_map/ppermute | solution.py:18
  170.6 8.2 %collective-permute-done.2 = bf16[8,32,384]{2,1,0:T(8,128)(2,1)S(1)} collective-permute-done((bf16[8,32,384]{2,1,0:T(8,128)(2,1)S(1)}, bf16[8,32,384]{2,1,0:T(8,128)(2,1)S(1)}, u32[]{:S(2)}, u32[]{:S(2)}) %collective-permute-start.2) | collective-permute-done | bytes 196640 | tf_op jit(solution)/shard_map/ppermute | solution.py:16
  179.6 2.4 gather_fusion.4
  182.0 4.2 %pad_maximum_fusion = bf16[24,256,384]{2,1,0:T(8,128)(2,1)} fusion(bf16[8,256,384]{2,1,0:T(8,128)(2,1)} %collective-permute-done.5, bf16[8,256,384]{2,1,0:T(8,128)(2,1)} %all-gather.2.cloned.1.call-done, bf16[8,256,384]{2,1,0:T(8,128)(2,1)} %collective-permute-done.4), kind=kLoop, calls=%fused_computation.5 | loop fusion | flops 4718592 | bytes 9437184 | tf_op jit(solution)/shard_map/concatenate | solution.py:14
  186.2 4.8 %gather_fusion = bf16[12,256,384]{2,1,0:T(8,128)(2,1)} fusion(bf16[24,256,384]{2,1,0:T(8,128)(2,1)} %pad_maximum_fusion, s32[1024]{0:T(1024)S(1)} %pad_clamp_fusion), kind=kCustom, calls=%fused_computation.2 | custom fusion | bytes 4718640 | tf_op jit(solution)/shard_map/jit(_take)/gather | solution.py:57
  191.0 5.3 %fusion.9 = bf16[2,6,256,256]{3,2,1,0:T(8,128)(2,1)} fusion(bf16[2,6,384,384]{3,2,1,0:T(8,128)(2,1)S(1)} %copy-done, bf16[2,6,256,384]{3,2,1,0:T(8,128)(2,1)} %bitcast.58, pred[2,6]{1,0:T(4,128)(4,1)S(1)} %get-tuple-element.3, bf16[2,256,384]{2,1,0:T(8,128)(2,1)} %param.11), kind=kOutput, calls=%fused_computation.11 | convolution fusion | flops 1513095168 | bytes 7864332 | tf_op jit(solution)/shard_map/gtco,gdo->gtcd/dot_general | solution.py:61
  198.1 17.5 %copy.11 = f32[2,256,256]{0,2,1:T(8,128)} copy(f32[2,256,256]{2,1,0:T(8,128)} %fusion.34) | data formatting | bytes 1048576 | tf_op jit(solution)/shard_map/convert_element_type | solution.py:64
  215.6 3.0 %gather_fusion.1 = f32[256,2]{1,0:T(8,128)} fusion(f32[2,256,256]{0,2,1:T(8,128)} %copy.11, s32[256]{0:T(256)S(1)} %bitcast.57), kind=kCustom, calls=%fused_computation.3 | custom fusion | bytes 6144 | tf_op jit(solution)/shard_map/jit(diagonal)/gather | solution.py:64
  219.5 2.6 %fusion.42 = (bf16[2,32,256]{2,1,0:T(8,128)(2,1)}, f32[2,32,256]{2,1,0:T(8,128)}) fusion(f32[2,256]{1,0:T(2,128)S(1)} %copy.12, bf16[2,256,384]{2,1,0:T(8,128)(2,1)} %param.11, f32[2,32,384]{2,1,0:T(8,128)} %param.7, bf16[2,6,384,384]{3,2,1,0:T(8,128)(2,1)S(1)} %copy-done, bf16[2,6,32,384]{3,2,1,0:T(8,128)(2,1)} %bitcast.59, ...), kind=kOutput, calls=%fused_computation.43 | convolution fusion | flops 126074880 | bytes 4425740 | tf_op jit(solution)/shard_map/gri,gci->grc/dot_general | solution.py:65
  222.1 6.7 %all_gather.15 = bf16[8,32,256]{2,1,0:T(8,128)(2,1)S(1)} all-gather(bf16[2,32,256]{2,1,0:T(8,128)(2,1)} %get-tuple-element.9), channel_id=1, replica_groups=mesh['slab'=128,'col'=4] {'col'}, dimensions={0}, use_global_device_ids=true | all-gather | bytes 163840 | tf_op jit(solution)/shard_map/all_gather | solution.py:26
  228.9 2.5 collective-permute-start.7
  231.4 4.3 %collective-permute-start.6 = (bf16[8,32,256]{2,1,0:T(8,128)(2,1)S(1)}, bf16[8,32,256]{2,1,0:T(8,128)(2,1)S(1)}, u32[]{:S(2)}, u32[]{:S(2)}) collective-permute-start(bf16[8,32,256]{2,1,0:T(8,128)(2,1)S(1)} %all_gather.15), channel_id=1, source_target_pairs={{0,4},{4,8},{8,12},{12,16},{16,20},{20,24},{24,28},{28,32},{32,36}... | collective-permute-start | bytes 393224 | tf_op jit(solution)/shard_map/ppermute | solution.py:16
  237.2 6.4 %collective-permute-done.6 = bf16[8,32,256]{2,1,0:T(8,128)(2,1)S(1)} collective-permute-done((bf16[8,32,256]{2,1,0:T(8,128)(2,1)S(1)}, bf16[8,32,256]{2,1,0:T(8,128)(2,1)S(1)}, u32[]{:S(2)}, u32[]{:S(2)}) %collective-permute-start.6) | collective-permute-done | bytes 131104 | tf_op jit(solution)/shard_map/ppermute | solution.py:16
  244.4 2.2 gather_fusion.2
  (24 shorter events, 20.6 us)
Async XLA Ops:
  7.2 144.1 %copy-start = (bf16[2,6,384,384]{3,2,1,0:T(8,128)(2,1)S(1)}, bf16[2,6,384,384]{3,2,1,0:T(8,128)(2,1)}, u32[]{:S(2)}) copy-start(bf16[2,6,384,384]{3,2,1,0:T(8,128)(2,1)} %param.8) | copy-start | bytes 10616836
  7.2 41.1 %all-gather.2.cloned.1.call-start = ((), (), s32[]{:S(2)}) async-start(), calls=%async_computation | async-start | bytes 1966080 | tf_op jit(solution)/shard_map/all_gather | solution.py:55
  48.3 133.8 %collective-permute-start.5 = (bf16[8,256,384]{2,1,0:T(8,128)(2,1)}, bf16[8,256,384]{2,1,0:T(8,128)(2,1)}, u32[]{:S(2)}, u32[]{:S(2)}) collective-permute-start(bf16[8,256,384]{2,1,0:T(8,128)(2,1)} %all-gather.2.cloned.1.call-done), channel_id=1, source_target_pairs={{4,0},{8,4},{12,8},{16,12},{20,16},{24,20},{28,24},{32,28},{36,32}... | collective-permute-start | bytes 4718600 | tf_op jit(solution)/shard_map/ppermute | solution.py:18
  58.2 123.8 %collective-permute-start.4 = (bf16[8,256,384]{2,1,0:T(8,128)(2,1)}, bf16[8,256,384]{2,1,0:T(8,128)(2,1)}, u32[]{:S(2)}, u32[]{:S(2)}) collective-permute-start(bf16[8,256,384]{2,1,0:T(8,128)(2,1)} %all-gather.2.cloned.1.call-done), channel_id=1, source_target_pairs={{0,4},{4,8},{8,12},{12,16},{16,20},{20,24},{24,28},{28,32},{32,36}... | collective-permute-start | bytes 4718600 | tf_op jit(solution)/shard_map/ppermute | solution.py:16
  124.9 12.5 %collective-permute-start.1 = (bf16[8,32,384]{2,1,0:T(8,128)(2,1)}, bf16[8,32,384]{2,1,0:T(8,128)(2,1)}, u32[]{:S(2)}, u32[]{:S(2)}) collective-permute-start(bf16[8,32,384]{2,1,0:T(8,128)(2,1)} %all_gather.12), channel_id=1, source_target_pairs={{4,0},{8,4},{12,8},{16,12},{20,16},{24,20},{28,24},{32,28},{36,32}... | collective-permute-start | bytes 589832 | tf_op jit(solution)/shard_map/ppermute | solution.py:18
  132.9 14.0 %collective-permute-start = (bf16[8,32,384]{2,1,0:T(8,128)(2,1)}, bf16[8,32,384]{2,1,0:T(8,128)(2,1)}, u32[]{:S(2)}, u32[]{:S(2)}) collective-permute-start(bf16[8,32,384]{2,1,0:T(8,128)(2,1)} %all_gather.12), channel_id=1, source_target_pairs={{0,4},{4,8},{8,12},{12,16},{16,20},{20,24},{24,28},{28,32},{32,36}... | collective-permute-start | bytes 589832 | tf_op jit(solution)/shard_map/ppermute | solution.py:16
  160.9 9.7 %collective-permute-start.3 = (bf16[8,32,384]{2,1,0:T(8,128)(2,1)S(1)}, bf16[8,32,384]{2,1,0:T(8,128)(2,1)S(1)}, u32[]{:S(2)}, u32[]{:S(2)}) collective-permute-start(bf16[8,32,384]{2,1,0:T(8,128)(2,1)S(1)} %all_gather.13), channel_id=1, source_target_pairs={{4,0},{8,4},{12,8},{16,12},{20,16},{24,20},{28,24},{32,28},{36,32}... | collective-permute-start | bytes 589832 | tf_op jit(solution)/shard_map/ppermute | solution.py:18
  165.1 13.6 %collective-permute-start.2 = (bf16[8,32,384]{2,1,0:T(8,128)(2,1)S(1)}, bf16[8,32,384]{2,1,0:T(8,128)(2,1)S(1)}, u32[]{:S(2)}, u32[]{:S(2)}) collective-permute-start(bf16[8,32,384]{2,1,0:T(8,128)(2,1)S(1)} %all_gather.13), channel_id=1, source_target_pairs={{0,4},{4,8},{8,12},{12,16},{16,20},{20,24},{24,28},{28,32},{32,36}... | collective-permute-start | bytes 589832 | tf_op jit(solution)/shard_map/ppermute | solution.py:16
  228.9 8.3 %collective-permute-start.7 = (bf16[8,32,256]{2,1,0:T(8,128)(2,1)S(1)}, bf16[8,32,256]{2,1,0:T(8,128)(2,1)S(1)}, u32[]{:S(2)}, u32[]{:S(2)}) collective-permute-start(bf16[8,32,256]{2,1,0:T(8,128)(2,1)S(1)} %all_gather.15), channel_id=1, source_target_pairs={{4,0},{8,4},{12,8},{16,12},{20,16},{24,20},{28,24},{32,28},{36,32}... | collective-permute-start | bytes 393224 | tf_op jit(solution)/shard_map/ppermute | solution.py:18
  231.4 12.2 %collective-permute-start.6 = (bf16[8,32,256]{2,1,0:T(8,128)(2,1)S(1)}, bf16[8,32,256]{2,1,0:T(8,128)(2,1)S(1)}, u32[]{:S(2)}, u32[]{:S(2)}) collective-permute-start(bf16[8,32,256]{2,1,0:T(8,128)(2,1)S(1)} %all_gather.15), channel_id=1, source_target_pairs={{0,4},{4,8},{8,12},{12,16},{16,20},{20,24},{24,28},{28,32},{32,36}... | collective-permute-start | bytes 393224 | tf_op jit(solution)/shard_map/ppermute | solution.py:16
  248.4 1.9 copy-start.1
Sparse Core Ops, SparseCore 0:
  10.1 38.1 all-gather.1
where the time goes:
time: 258 us; the launch traced here: 257 us
  blocking collectives  76.4 us (30%)
  waiting for transfers between devices  71.2 us (28%)
  starting transfers between devices  35.4 us (14%)
  local copies, waits for them, and re-layouts  33.3 us (13%)
  matrix products  16.3 us (6%)
  between operations  14.1 us (5%)
  other arithmetic  10.4 us (4%)
    all_gather x3, blocking collectives, neighbour_rows(): slab_rows = lax.all_gather(vec_rounded, 'col', axis=0, tiled=True)  76.4 us
    all_gather x1, waiting for transfers between devices, per_device(): wide_basis = lax.all_gather(basis, 'col', axis=0, tiled=True)  40.4 us
    ppermute x4, starting transfers between devices, with_halo(): lax.ppermute(head, axis, [((i + 1) % count, i) for i in range(count)])  24.7 us
    ppermute x4, waiting for transfers between devices, with_halo(): lax.ppermute(tail, axis, [(i, (i + 1) % count) for i in range(count)])  24.1 us
    convert_element_type x1, local copies, waits for them, and re-layouts, per_device(): coarse_tiles[:, 0].astype(jnp.float32)  17.5 us
    ppermute x4, starting transfers between devices, with_halo(): lax.ppermute(tail, axis, [(i, (i + 1) % count) for i in range(count)])  10.7 us
    concatenate x4, other arithmetic, with_halo(): jnp.concatenate([lax.ppermute(tail, axis, [(i, (i + 1) % count) for i in...  7.86 us
    ppermute x4, waiting for transfers between devices, with_halo(): lax.ppermute(head, axis, [((i + 1) % count, i) for i in range(count)])  6.03 us
  transfers between devices with their start and end apart: 9, of which 7 were waited for; matrix products, arithmetic and copies ran while one was open for 5% of the time, Pallas kernels for 0%

commit v1 on v0

v1 whole, which is shorter than its diff:
```python
import functools

import jax
import jax.numpy as jnp
from jax import lax
from jax.experimental import pallas as pl
from jax.experimental.pallas import tpu as pltpu
from jax.sharding import PartitionSpec as P

damping = 0.8
AXES = ("slab", "col")
VMEM = pltpu.VMEM
bf16 = jnp.bfloat16
f32 = jnp.float32


def dot(a, b):
    return jnp.dot(a, b, preferred_element_type=f32)


def dot_t(a, b):
    return lax.dot_general(a, b, (((1,), (1,)), ((), ())), preferred_element_type=f32)


def split(value):
    high = value.astype(bf16)
    return high, (value - high.astype(f32)).astype(bf16)


def pairs(slabs, cols, partner):
    groups = []
    for s in range(slabs):
        for c in range(cols):
            s2, c2 = partner(s, c)
            i, j = s * cols + c, (s2 % slabs) * cols + c2
            if i < j:
                groups.append([i, j])
    return groups


def exchange(cells, slabs, cols):
    def crossing(s, c):
        even = s % 2 == 0
        up = even == (c % 2 == 0)
        return (s + 1 if up else s - 1), c ^ 2

    def send(s, c):
        s2, c2 = crossing(s, c)
        return s * cols + c, (s2 % slabs) * cols + c2

    own = lax.all_gather(cells, "col", axis=0, tiled=True)
    beside = lax.ppermute(
        own, AXES, [send(s, c) for s in range(slabs) for c in range(cols)]
    )
    halo = lax.all_gather(
        beside,
        AXES,
        axis=0,
        tiled=True,
        axis_index_groups=pairs(slabs, cols, lambda s, c: (s, c ^ 1)),
    )
    return own, halo


def pick(own, halo, cell, here, slab_cells):
    slab = lax.div(cell, slab_cells)
    offset = lax.rem(cell, slab_cells)
    inside = lax.div(slab, 2) == lax.div(here, 2)
    there = halo[jnp.where(inside, offset, slab_cells + offset)]
    return jnp.where(slab == here, own[offset], there)


def fetch(tiles_hbm, tiles, sems, first=0):
    copies = {}
    for t in range(first, tiles.shape[1]):
        for g in range(tiles.shape[0]):
            copies[g, t] = pltpu.make_async_copy(
                tiles_hbm.at[g, t], tiles.at[g, t], sems.at[g, t]
            )
            copies[g, t].start()
    return copies


def apply_tiles(own, halo, nb, tiles, copies, slab_cells, first=0):
    here = lax.axis_index("slab")
    cells, kinds = tiles.shape[0], tiles.shape[1]
    sums = [None] * cells
    for t in range(first, kinds):
        for g in range(cells):
            copies[g, t].wait()
            part = dot(pick(own, halo, nb[g, t], here, slab_cells), tiles[g, t])
            sums[g] = part if sums[g] is None else sums[g] + part
    return sums


def first_body(rhs, own_tiles, smoother, basis, x_out, xb_out, coarse_out, pivot_out):
    for g in range(rhs.shape[0]):
        x = dot(rhs[g].astype(bf16), smoother[g])
        x_out[g] = x
        xb_out[g] = x.astype(bf16)
    size = basis.shape[1]
    eye = lax.broadcasted_iota(jnp.int32, (size, size), 0) == lax.broadcasted_iota(
        jnp.int32, (size, size), 1
    )
    for g in range(rhs.shape[0]):
        upper = dot(basis[g], own_tiles[g, 0]).astype(bf16)
        coarse = dot_t(upper, basis[g]).astype(bf16)
        coarse_out[g] = coarse
        pivot_out[g] = jnp.sum(
            jnp.where(eye, coarse.astype(f32), 0.0), axis=0, keepdims=True
        )


def second_body(slab_cells, nb, mine, halo, rhs, x_first, smoother, tiles_hbm, x_out, xb_out, tiles, sems):
    copies = fetch(tiles_hbm, tiles, sems)
    sums = apply_tiles(mine, halo, nb, tiles, copies, slab_cells)
    for g, image in enumerate(sums):
        x = x_first[g] + dot((rhs[g] - image).astype(bf16), smoother[g])
        x_out[g] = x
        xb_out[g] = x.astype(bf16)


def third_body(
    slab_cells, nb, mine, halo, rhs, basis, coarse, pivot, tiles_hbm, base_out, fine_out, tiles, sems
):
    copies = fetch(tiles_hbm, tiles, sems)
    sums = apply_tiles(mine, halo, nb, tiles, copies, slab_cells)
    rows = rhs.shape[1]
    for g, image in enumerate(sums):
        coarse_rhs = dot_t((rhs[g] - image).astype(bf16), basis[g])
        c_first = damping * coarse_rhs / pivot[g]
        rounded = c_first.astype(bf16)
        own = dot(rounded, coarse[g])
        base_out[g] = c_first + damping * (coarse_rhs - own) / pivot[g]
        high, low = split(dot(rounded, basis[g]))
        fine_out[g, :rows] = high
        fine_out[g, rows:] = low


def fourth_body(
    slab_cells, nb, mine, halo, base, x_second, basis, pivot, tiles_hbm, sol_out, iter_out, tiles, sems
):
    copies = fetch(tiles_hbm, tiles, sems, 1)
    sums = apply_tiles(mine, halo, nb, tiles, copies, slab_cells, 1)
    rows = x_second.shape[1]
    for g, image in enumerate(sums):
        high, low = split(image[:rows] + image[rows:])
        rest = dot_t(high, basis[g]) + dot_t(low, basis[g])
        iterate = base[g] - damping * rest / pivot[g]
        iter_out[g] = iterate
        sol_out[g] = x_second[g] + dot(iterate.astype(bf16), basis[g])


def call(body, outs, specs, scratch=()):
    return pl.pallas_call(
        body,
        out_shape=outs,
        in_specs=specs,
        out_specs=tuple(pl.BlockSpec(memory_space=VMEM) for _ in outs),
        scratch_shapes=list(scratch),
        compiler_params=pltpu.CompilerParams(vmem_limit_bytes=24 * 2**20),
    )


def per_device(slabs, cols, rhs, tiles, neighbours, smoother, basis):
    cells, rows, block = rhs.shape
    kinds, size = tiles.shape[1], basis.shape[1]
    slab_cells = cells * cols
    shape = jax.ShapeDtypeStruct
    vmem = pl.BlockSpec(memory_space=VMEM)
    smem = pl.BlockSpec(memory_space=pltpu.SMEM)
    anywhere = pl.BlockSpec(memory_space=pl.ANY)
    held = (
        pltpu.VMEM((cells, kinds, block, block), bf16),
        pltpu.SemaphoreType.DMA((cells, kinds)),
    )
    x_first, send, coarse, pivot = pl.pallas_call(
        first_body,
        grid=(1,),
        out_shape=(
            shape((cells, rows, block), f32),
            shape((cells, rows, block), bf16),
            shape((cells, size, size), bf16),
            shape((cells, 1, size), f32),
        ),
        in_specs=[
            vmem,
            pl.BlockSpec((cells, 1, block, block), lambda i: (0, 0, 0, 0)),
            vmem,
            vmem,
        ],
        out_specs=(vmem, vmem, vmem, vmem),
        compiler_params=pltpu.CompilerParams(vmem_limit_bytes=24 * 2**20),
    )(rhs, tiles, smoother, basis)
    near = exchange(send, slabs, cols)
    x_second, send = call(
        functools.partial(second_body, slab_cells),
        (shape((cells, rows, block), f32), shape((cells, rows, block), bf16)),
        [smem, vmem, vmem, vmem, vmem, vmem, anywhere],
        held,
    )(neighbours, *near, rhs, x_first, smoother, tiles)
    near = exchange(send, slabs, cols)
    base, send = call(
        functools.partial(third_body, slab_cells),
        (shape((cells, rows, size), f32), shape((cells, 2 * rows, block), bf16)),
        [smem, vmem, vmem, vmem, vmem, vmem, vmem, anywhere],
        held,
    )(neighbours, *near, rhs, basis, coarse, pivot, tiles)
    near = exchange(send, slabs, cols)
    return call(
        functools.partial(fourth_body, slab_cells),
        (shape((cells, rows, block), f32), shape((cells, rows, size), f32)),
        [smem, vmem, vmem, vmem, vmem, vmem, vmem, anywhere],
        held,
    )(neighbours, *near, base, x_second, basis, pivot, tiles)


def solution(mesh):
    placed = (
        P(AXES, None, None),
        P(AXES, None, None, None),
        P(AXES, None),
        P(AXES, None, None),
        P(AXES, None, None),
    )
    return jax.shard_map(
        functools.partial(per_device, mesh.shape["slab"], mesh.shape["col"]),
        mesh=mesh,
        in_specs=placed,
        out_specs=(P(AXES, None, None), P(AXES, None, None)),
        check_vma=False,
    )
```

time: 258 us -> 89 us (0.34)
  waiting for transfers between devices: 71.2 us -> 11.3 us
  blocking collectives: 76.4 us -> 31.9 us
  local copies, waits for them, and re-layouts: 33.3 us -> 4.96 us
  matrix products: 16.3 us -> 0 us
  between operations: 14.1 us -> 0.7 us
  Pallas kernels: 0 us -> 11.5 us
  other arithmetic: 10.4 us -> 0 us
  starting transfers between devices: 35.4 us -> 28.2 us
    all_gather x3 -> x6, blocking collectives: 76.4 us -> 31.9 us  [the longest x3 24.5 us: exchange(): own = lax.all_gather(cells, 'col', axis=0, tiled=True)]
    all_gather x1 -> x0, waiting for transfers between devices: 40.4 us -> none  [per_device(): wide_basis = lax.all_gather(basis, 'col', axis=0, tiled=True)]
    ppermute x8 -> x3, waiting for transfers between devices: 30.2 us -> 11.3 us  [exchange(): lax.ppermute(own, AXES, [send(s, c) for s in range(slabs) for c in range(...]
    convert_element_type x1 -> x0, local copies, waits for them, and re-layouts: 17.5 us -> none  [per_device(): coarse_tiles[:, 0].astype(jnp.float32)]
    dot_general x6 -> x0, matrix products: 16.3 us -> none  [the longest x1 5.33 us: per_device(): jnp.einsum('gtco,gdo->gtcd', upper, basis, preferred_element_type=jnp.flo...]
    gather x6 -> x0, local copies, waits for them, and re-layouts: 15.7 us -> none  [the longest x1 4.78 us: per_device(): picked_basis = jnp.take(near_basis, row_place, axis=0)]
    pallas_call x0 -> x4, Pallas kernels: none -> 11.5 us  [the longest x1 3.99 us: per_device(): call(functools.partial(fourth_body, slab_cells), (shape((cells, rows, blo...]
    concatenate x5 -> x0, other arithmetic: 7.87 us -> none  [the longest x4 7.86 us: with_halo(): jnp.concatenate([lax.ppermute(tail, axis, [(i, (i + 1) % count) for i in...]
  transfers between devices with their start and end apart: 9 -> 3, of which waited for: 7 -> 3; matrix products, arithmetic and copies ran while one was open for 5% -> 0% of each run, Pallas kernels for 0% -> 0%
where the time goes in v1:
time: 89 us; the launch traced here: 88.6 us
  blocking collectives  31.9 us (36%)
  starting transfers between devices  28.2 us (32%)
  Pallas kernels  11.5 us (13%)
  waiting for transfers between devices  11.3 us (13%)
  local copies, waits for them, and re-layouts  4.96 us (6%)
    ppermute x3, starting transfers between devices, exchange(): lax.ppermute(own, AXES, [send(s, c) for s in range(slabs) for c in range(...  28.2 us
    all_gather x3, blocking collectives, exchange(): own = lax.all_gather(cells, 'col', axis=0, tiled=True)  24.5 us
    ppermute x3, waiting for transfers between devices, exchange(): lax.ppermute(own, AXES, [send(s, c) for s in range(slabs) for c in range(...  11.3 us
    all_gather x3, blocking collectives, exchange(): lax.all_gather(beside, AXES, axis=0, tiled=True, axis_index_groups=pairs(...  7.34 us
    unnamed x14, local copies, waits for them, and re-layouts  4.96 us
    pallas_call x1, Pallas kernels, per_device(): call(functools.partial(fourth_body, slab_cells), (shape((cells, rows, blo...  3.99 us
    pallas_call x1, Pallas kernels, per_device(): call(functools.partial(third_body, slab_cells), (shape((cells, rows, size...  3.51 us
    pallas_call x1, Pallas kernels, per_device(): call(functools.partial(second_body, slab_cells), (shape((cells, rows, blo...  3.12 us
  transfers between devices with their start and end apart: 3, of which 3 were waited for; matrix products, arithmetic and copies ran while one was open for 0% of the time, Pallas kernels for 0%

profile of v1, /device:TPU:1, one launch (start us, length us, event | category | flops | bytes accessed | tf_op | source)
XLA Modules:
  0.0 88.6 jit_solution(8236646708047434748)
XLA Ops:
  0.6 0.0 copy-start
  0.6 2.0 %copy-done = bf16[2,6,384,384]{3,2,1,0:T(8,128)(2,1)S(1)} copy-done((bf16[2,6,384,384]{3,2,1,0:T(8,128)(2,1)S(1)}, bf16[2,6,384,384]{3,2,1,0:T(8,128)(2,1)}, u32[]{:S(2)}) %copy-start) | copy-done | bytes 3538968
  2.6 1.0 %copy-done.2 = bf16[2,256,384]{2,1,0:T(8,128)(2,1)S(1)} copy-done((bf16[2,256,384]{2,1,0:T(8,128)(2,1)S(1)}, bf16[2,256,384]{2,1,0:T(8,128)(2,1)}, u32[]{:S(2)}) %copy-start.2) | copy-done | bytes 393240
  3.6 1.1 %copy-done.4 = bf16[2,384,384]{2,1,0:T(8,128)(2,1)S(1)} copy-done((bf16[2,384,384]{2,1,0:T(8,128)(2,1)S(1)}, bf16[2,384,384]{2,1,0:T(8,128)(2,1)}, u32[]{:S(2)}) %copy-start.4) | copy-done | bytes 589848
  4.7 0.9 %copy-done.5 = f32[2,32,384]{2,1,0:T(8,128)S(1)} copy-done((f32[2,32,384]{2,1,0:T(8,128)S(1)}, f32[2,32,384]{2,1,0:T(8,128)}, u32[]{:S(2)}) %copy-start.5) | copy-done | bytes 98328
  5.6 0.9 shard_map.68
  6.5 0.0 copy-start.3
  6.5 12.4 %all_gather.18.mine = bf16[8,32,384]{2,1,0:T(8,128)(2,1)S(1)} all-gather(bf16[2,32,384]{2,1,0:T(8,128)(2,1)S(1)} %get-tuple-element.10), channel_id=1, replica_groups=mesh['slab'=128,'col'=4] {'col'}, dimensions={0}, use_global_device_ids=true | all-gather | bytes 245760 | tf_op jit(solution)/shard_map/all_gather | solution.py:51
  18.9 10.4 %collective-permute-start = (bf16[8,32,384]{2,1,0:T(8,128)(2,1)S(1)}, bf16[8,32,384]{2,1,0:T(8,128)(2,1)S(1)}, u32[]{:S(2)}, u32[]{:S(2)}) collective-permute-start(bf16[8,32,384]{2,1,0:T(8,128)(2,1)S(1)} %all_gather.18.mine), channel_id=1, source_target_pairs={{0,6},{1,511},{2,4},{3,509},{4,2},{5,11},{6,0},{7,9},{8,14},{9,7},... | collective-permute-start | bytes 589832 | tf_op jit(solution)/shard_map/ppermute | solution.py:52
  29.3 3.0 %collective-permute-done = bf16[8,32,384]{2,1,0:T(8,128)(2,1)S(1)} collective-permute-done((bf16[8,32,384]{2,1,0:T(8,128)(2,1)S(1)}, bf16[8,32,384]{2,1,0:T(8,128)(2,1)S(1)}, u32[]{:S(2)}, u32[]{:S(2)}) %collective-permute-start) | collective-permute-done | bytes 196640 | tf_op jit(solution)/shard_map/ppermute | solution.py:52
  32.3 2.1 %all_gather.19.halo = bf16[16,32,384]{2,1,0:T(8,128)(2,1)S(1)} all-gather(bf16[8,32,384]{2,1,0:T(8,128)(2,1)S(1)} %collective-permute-done), channel_id=1, replica_groups={{0,1},{2,3},{4,5},{6,7},{8,9},{10,11},{12,13},{14,15},{16,17},{18,19},{..., dimensions={0}, use_global_device_ids=true | all-gather | bytes 589824 | tf_op jit(solution)/shard_map/all_gather | solution.py:55
  34.4 0.0 copy-done.6
  34.4 3.1 %shard_map.69 = (f32[2,32,384]{2,1,0:T(8,128)S(1)}, bf16[2,32,384]{2,1,0:T(8,128)(2,1)S(1)}) custom-call(s32[2,6]{1,0:T(2,128)S(1)} %copy-done.6, bf16[8,32,384]{2,1,0:T(8,128)(2,1)S(1)} %all_gather.18.mine, bf16[16,32,384]{2,1,0:T(8,128)(2,1)S(1)} %all_gather.19.halo, f32[2,32,384]{2,1,0:T(8,128)S(1)} %copy-done.5, ...), custom_call_target="tpu_custom_call" | custom-call | tf_op jit(solution)/shard_map/pallas_call | solution.py:196
  37.5 5.6 %all_gather.20.mine = bf16[8,32,384]{2,1,0:T(8,128)(2,1)S(1)} all-gather(bf16[2,32,384]{2,1,0:T(8,128)(2,1)S(1)} %get-tuple-element.12), channel_id=1, replica_groups=mesh['slab'=128,'col'=4] {'col'}, dimensions={0}, use_global_device_ids=true | all-gather | bytes 245760 | tf_op jit(solution)/shard_map/all_gather | solution.py:51
  43.1 9.0 %collective-permute-start.1 = (bf16[8,32,384]{2,1,0:T(8,128)(2,1)S(1)}, bf16[8,32,384]{2,1,0:T(8,128)(2,1)S(1)}, u32[]{:S(2)}, u32[]{:S(2)}) collective-permute-start(bf16[8,32,384]{2,1,0:T(8,128)(2,1)S(1)} %all_gather.20.mine), channel_id=1, source_target_pairs={{0,6},{1,511},{2,4},{3,509},{4,2},{5,11},{6,0},{7,9},{8,14},{9,7},... | collective-permute-start | bytes 589832 | tf_op jit(solution)/shard_map/ppermute | solution.py:52
  52.2 3.0 %collective-permute-done.1 = bf16[8,32,384]{2,1,0:T(8,128)(2,1)S(1)} collective-permute-done((bf16[8,32,384]{2,1,0:T(8,128)(2,1)S(1)}, bf16[8,32,384]{2,1,0:T(8,128)(2,1)S(1)}, u32[]{:S(2)}, u32[]{:S(2)}) %collective-permute-start.1) | collective-permute-done | bytes 196640 | tf_op jit(solution)/shard_map/ppermute | solution.py:52
  55.2 2.1 %all_gather.21.halo = bf16[16,32,384]{2,1,0:T(8,128)(2,1)S(1)} all-gather(bf16[8,32,384]{2,1,0:T(8,128)(2,1)S(1)} %collective-permute-done.1), channel_id=1, replica_groups={{0,1},{2,3},{4,5},{6,7},{8,9},{10,11},{12,13},{14,15},{16,17},{18,19},{..., dimensions={0}, use_global_device_ids=true | all-gather | bytes 589824 | tf_op jit(solution)/shard_map/all_gather | solution.py:55
  57.3 0.0 copy-done.3
  57.3 3.5 %shard_map.70 = (f32[2,32,256]{2,1,0:T(8,128)S(1)}, bf16[2,64,384]{2,1,0:T(8,128)(2,1)S(1)}) custom-call(s32[2,6]{1,0:T(2,128)S(1)} %copy-done.6, bf16[8,32,384]{2,1,0:T(8,128)(2,1)S(1)} %all_gather.20.mine, bf16[16,32,384]{2,1,0:T(8,128)(2,1)S(1)} %all_gather.21.halo, f32[2,32,384]{2,1,0:T(8,128)S(1)} %copy-done.5, bf16[2,256,384]{2,1,0:T(8,128)(2,1)S(1)} %copy-done.3, ...), custom_call_target="tpu_custom_call" | custom-call | tf_op jit(solution)/shard_map/pallas_call | solution.py:203
  60.8 6.6 %all_gather.22.mine = bf16[8,64,384]{2,1,0:T(8,128)(2,1)S(1)} all-gather(bf16[2,64,384]{2,1,0:T(8,128)(2,1)S(1)} %get-tuple-element.15), channel_id=1, replica_groups=mesh['slab'=128,'col'=4] {'col'}, dimensions={0}, use_global_device_ids=true | all-gather | bytes 491520 | tf_op jit(solution)/shard_map/all_gather | solution.py:51
  67.4 8.8 %collective-permute-start.2 = (bf16[8,64,384]{2,1,0:T(8,128)(2,1)S(1)}, bf16[8,64,384]{2,1,0:T(8,128)(2,1)S(1)}, u32[]{:S(2)}, u32[]{:S(2)}) collective-permute-start(bf16[8,64,384]{2,1,0:T(8,128)(2,1)S(1)} %all_gather.22.mine), channel_id=1, source_target_pairs={{0,6},{1,511},{2,4},{3,509},{4,2},{5,11},{6,0},{7,9},{8,14},{9,7},... | collective-permute-start | bytes 1179656 | tf_op jit(solution)/shard_map/ppermute | solution.py:52
  76.2 5.3 %collective-permute-done.2 = bf16[8,64,384]{2,1,0:T(8,128)(2,1)S(1)} collective-permute-done((bf16[8,64,384]{2,1,0:T(8,128)(2,1)S(1)}, bf16[8,64,384]{2,1,0:T(8,128)(2,1)S(1)}, u32[]{:S(2)}, u32[]{:S(2)}) %collective-permute-start.2) | collective-permute-done | bytes 393248 | tf_op jit(solution)/shard_map/ppermute | solution.py:52
  81.4 3.2 %all_gather.23.halo = bf16[16,64,384]{2,1,0:T(8,128)(2,1)S(1)} all-gather(bf16[8,64,384]{2,1,0:T(8,128)(2,1)S(1)} %collective-permute-done.2), channel_id=1, replica_groups={{0,1},{2,3},{4,5},{6,7},{8,9},{10,11},{12,13},{14,15},{16,17},{18,19},{..., dimensions={0}, use_global_device_ids=true | all-gather | bytes 1179648 | tf_op jit(solution)/shard_map/all_gather | solution.py:55
  84.6 4.0 %shard_map.71 = (f32[2,32,384]{2,1,0:T(8,128)}, f32[2,32,256]{2,1,0:T(8,128)}) custom-call(s32[2,6]{1,0:T(2,128)S(1)} %copy-done.6, bf16[8,64,384]{2,1,0:T(8,128)(2,1)S(1)} %all_gather.22.mine, bf16[16,64,384]{2,1,0:T(8,128)(2,1)S(1)} %all_gather.23.halo, f32[2,32,256]{2,1,0:T(8,128)S(1)} %get-tuple-element.16.base, ...), custom_call_target="tpu_custom_call" | custom-call | tf_op jit(solution)/shard_map/pallas_call | solution.py:210
  (6 shorter events, 0.0 us)
Async XLA Ops:
  0.6 2.0 %copy-start = (bf16[2,6,384,384]{3,2,1,0:T(8,128)(2,1)S(1)}, bf16[2,6,384,384]{3,2,1,0:T(8,128)(2,1)}, u32[]{:S(2)}) copy-start(bf16[2,6,384,384]{3,2,1,0:T(8,128)(2,1)} %tiles_hbm.5) | copy-start | bytes 10616836
  2.6 1.0 %copy-start.2 = (bf16[2,256,384]{2,1,0:T(8,128)(2,1)S(1)}, bf16[2,256,384]{2,1,0:T(8,128)(2,1)}, u32[]{:S(2)}) copy-start(bf16[2,256,384]{2,1,0:T(8,128)(2,1)} %basis.5) | copy-start | bytes 1179652
  3.6 1.1 %copy-start.4 = (bf16[2,384,384]{2,1,0:T(8,128)(2,1)S(1)}, bf16[2,384,384]{2,1,0:T(8,128)(2,1)}, u32[]{:S(2)}) copy-start(bf16[2,384,384]{2,1,0:T(8,128)(2,1)} %smoother.3) | copy-start | bytes 1769476
  4.7 0.9 %copy-start.5 = (f32[2,32,384]{2,1,0:T(8,128)S(1)}, f32[2,32,384]{2,1,0:T(8,128)}, u32[]{:S(2)}) copy-start(f32[2,32,384]{2,1,0:T(8,128)} %rhs.5) | copy-start | bytes 294916
  5.6 28.8 %copy-start.6 = (s32[2,6]{1,0:T(2,128)S(1)}, s32[2,6]{1,0:T(2,128)}, u32[]{:S(2)}) copy-start(s32[2,6]{1,0:T(2,128)} %nb.5) | copy-start | bytes 148
  6.5 50.8 %copy-start.3 = (bf16[2,256,384]{2,1,0:T(8,128)(2,1)S(1)}, bf16[2,256,384]{2,1,0:T(8,128)(2,1)}, u32[]{:S(2)}) copy-start(bf16[2,256,384]{2,1,0:T(8,128)(2,1)} %basis.5) | copy-start | bytes 1179652
  18.9 13.5 %collective-permute-start = (bf16[8,32,384]{2,1,0:T(8,128)(2,1)S(1)}, bf16[8,32,384]{2,1,0:T(8,128)(2,1)S(1)}, u32[]{:S(2)}, u32[]{:S(2)}) collective-permute-start(bf16[8,32,384]{2,1,0:T(8,128)(2,1)S(1)} %all_gather.18.mine), channel_id=1, source_target_pairs={{0,6},{1,511},{2,4},{3,509},{4,2},{5,11},{6,0},{7,9},{8,14},{9,7},... | collective-permute-start | bytes 589832 | tf_op jit(solution)/shard_map/ppermute | solution.py:52
  43.1 41.5 %copy-start.1 = (bf16[2,6,384,384]{3,2,1,0:T(8,128)(2,1)S(1)}, bf16[2,6,384,384]{3,2,1,0:T(8,128)(2,1)}, u32[]{:S(2)}) copy-start(bf16[2,6,384,384]{3,2,1,0:T(8,128)(2,1)} %tiles_hbm.5) | copy-start | bytes 10616836
  43.1 12.1 %collective-permute-start.1 = (bf16[8,32,384]{2,1,0:T(8,128)(2,1)S(1)}, bf16[8,32,384]{2,1,0:T(8,128)(2,1)S(1)}, u32[]{:S(2)}, u32[]{:S(2)}) collective-permute-start(bf16[8,32,384]{2,1,0:T(8,128)(2,1)S(1)} %all_gather.20.mine), channel_id=1, source_target_pairs={{0,6},{1,511},{2,4},{3,509},{4,2},{5,11},{6,0},{7,9},{8,14},{9,7},... | collective-permute-start | bytes 589832 | tf_op jit(solution)/shard_map/ppermute | solution.py:52
  67.4 14.0 %collective-permute-start.2 = (bf16[8,64,384]{2,1,0:T(8,128)(2,1)S(1)}, bf16[8,64,384]{2,1,0:T(8,128)(2,1)S(1)}, u32[]{:S(2)}, u32[]{:S(2)}) collective-permute-start(bf16[8,64,384]{2,1,0:T(8,128)(2,1)S(1)} %all_gather.22.mine), channel_id=1, source_target_pairs={{0,6},{1,511},{2,4},{3,509},{4,2},{5,11},{6,0},{7,9},{8,14},{9,7},... | collective-permute-start | bytes 1179656 | tf_op jit(solution)/shard_map/ppermute | solution.py:52

commit v2 on v1

v2 whole, which is shorter than its diff:
```python
import functools

import jax
import jax.numpy as jnp
from jax import lax
from jax.experimental import pallas as pl
from jax.experimental.pallas import tpu as pltpu
from jax.sharding import PartitionSpec as P

damping = 0.8
AXES = ("slab", "col")
VMEM = pltpu.VMEM
bf16 = jnp.bfloat16
f32 = jnp.float32


def dot(a, b):
    return jnp.dot(a, b, preferred_element_type=f32)


def dot_t(a, b):
    return lax.dot_general(a, b, (((1,), (1,)), ((), ())), preferred_element_type=f32)


def split(value):
    high = value.astype(bf16)
    return high, (value - high.astype(f32)).astype(bf16)


def pairs(slabs, cols, partner):
    groups = []
    for s in range(slabs):
        for c in range(cols):
            s2, c2 = partner(s, c)
            i, j = s * cols + c, (s2 % slabs) * cols + c2
            if i < j:
                groups.append([i, j])
    return groups


def gather(values, slabs, cols, flip):
    return lax.all_gather(
        values,
        AXES,
        axis=0,
        tiled=True,
        axis_index_groups=pairs(slabs, cols, lambda s, c: (s, c ^ flip)),
    )


def crossing(s, c, slabs):
    up = (s % 2 == 0) == (c % 2 == 0)
    return (s + 1 if up else s - 1) % slabs, c ^ 2


def cross(values, slabs, cols):
    def target(s, c):
        s2, c2 = crossing(s, c, slabs)
        return s2 * cols + c2

    return lax.ppermute(
        values,
        AXES,
        [(s * cols + c, target(s, c)) for s in range(slabs) for c in range(cols)],
    )


def exchange(cells, slabs, cols):
    chip = gather(cells, slabs, cols, 1)
    beside = cross(chip, slabs, cols)
    own = gather(chip, slabs, cols, 2)
    return own, lax.all_gather(beside, "col", axis=0, tiled=True)


def pick(near, cell, here, slab_cells):
    slab = lax.div(cell, slab_cells)
    offset = lax.rem(cell, slab_cells)
    half = slab_cells // 2
    chip, inner = lax.div(offset, half), lax.rem(offset, half)
    odd = jnp.where(lax.div(slab, 2) == lax.div(here, 2), 0, 1)
    col = 2 * (1 - chip) + odd
    own, halo = near
    return jnp.where(slab == here, own[offset], halo[col * half + inner])


def apply_tiles(near, nb, tiles, slab_cells, first=0):
    here = lax.axis_index("slab")
    cells, kinds = tiles.shape[0], tiles.shape[1]
    sums = [None] * cells
    for t in range(first, kinds):
        for g in range(cells):
            part = dot(pick(near, nb[g, t], here, slab_cells), tiles[g, t])
            sums[g] = part if sums[g] is None else sums[g] + part
    return sums


def first_body(*refs):
    sources, (x_out, xb_out, rhs, smoother, basis, tiles), sems = refs[:4], refs[4:10], refs[10]
    copies = []
    for k, (source, target) in enumerate(zip(sources, (smoother, rhs, tiles, basis))):
        for g in range(rhs.shape[0]):
            copy = pltpu.make_async_copy(source.at[g], target.at[g], sems.at[k, g])
            copy.start()
            copies.append(copy)
    for copy in copies[: 2 * rhs.shape[0]]:
        copy.wait()
    for g in range(rhs.shape[0]):
        x = dot(rhs[g].astype(bf16), smoother[g])
        x_out[g] = x
        xb_out[g] = x.astype(bf16)
    for copy in copies[2 * rhs.shape[0] :]:
        copy.wait()


def coarse_body(own_tiles, basis, coarse_out, pivot_out):
    size = basis.shape[1]
    eye = lax.broadcasted_iota(jnp.int32, (size, size), 0) == lax.broadcasted_iota(
        jnp.int32, (size, size), 1
    )
    for g in range(basis.shape[0]):
        upper = dot(basis[g], own_tiles[g, 0]).astype(bf16)
        coarse = dot_t(upper, basis[g]).astype(bf16)
        coarse_out[g] = coarse
        pivot_out[g] = jnp.sum(
            jnp.where(eye, coarse.astype(f32), 0.0), axis=0, keepdims=True
        )


def second_body(slab_cells, nb, rhs, x_first, smoother, tiles, *refs):
    *near, x_out, xb_out = refs
    sums = apply_tiles(near, nb, tiles, slab_cells)
    for g, image in enumerate(sums):
        x = x_first[g] + dot((rhs[g] - image).astype(bf16), smoother[g])
        x_out[g] = x
        xb_out[g] = x.astype(bf16)


def third_body(
    slab_cells, nb, rhs, basis, coarse, pivot, tiles, *refs
):
    *near, base_out, fine_out = refs
    sums = apply_tiles(near, nb, tiles, slab_cells)
    rows = rhs.shape[1]
    for g, image in enumerate(sums):
        coarse_rhs = dot_t((rhs[g] - image).astype(bf16), basis[g])
        c_first = damping * coarse_rhs / pivot[g]
        rounded = c_first.astype(bf16)
        own = dot(rounded, coarse[g])
        base_out[g] = c_first + damping * (coarse_rhs - own) / pivot[g]
        high, low = split(dot(rounded, basis[g]))
        fine_out[g, :rows] = high
        fine_out[g, rows:] = low


def fourth_body(
    slab_cells, nb, base, x_second, basis, pivot, tiles, *refs
):
    *near, sol_out, iter_out = refs
    sums = apply_tiles(near, nb, tiles, slab_cells, 1)
    rows = x_second.shape[1]
    for g, image in enumerate(sums):
        parts = jnp.concatenate(split(image[:rows] + image[rows:]))
        both = dot_t(parts, basis[g])
        rest = both[:rows] + both[rows:]
        iterate = base[g] - damping * rest / pivot[g]
        iter_out[g] = iterate
        sol_out[g] = x_second[g] + dot(iterate.astype(bf16), basis[g])


def call(body, outs, specs, scratch=(), limit=24 * 2**20, moved=None):
    return pl.pallas_call(
        body,
        out_shape=outs,
        in_specs=specs,
        out_specs=tuple(pl.BlockSpec(memory_space=VMEM) for _ in outs),
        scratch_shapes=list(scratch),
        compiler_params=pltpu.CompilerParams(vmem_limit_bytes=limit),
        cost_estimate=moved
        and pl.CostEstimate(flops=0, transcendentals=0, bytes_accessed=moved),
    )


def per_device(slabs, cols, rhs, tiles, neighbours, smoother, basis):
    cells, rows, block = rhs.shape
    size = basis.shape[1]
    slab_cells = cells * cols
    shape = jax.ShapeDtypeStruct
    vmem = pl.BlockSpec(memory_space=VMEM)
    hbm = pl.BlockSpec(memory_space=pltpu.HBM)
    smem = pl.BlockSpec(memory_space=pltpu.SMEM)
    fixed = [
        pltpu.with_memory_space_constraint(v, pltpu.HBM) for v in (smoother, rhs, tiles, basis)
    ]
    x_first, send, rhs, smoother, basis, tiles = call(
        first_body,
        (shape((cells, rows, block), f32), shape((cells, rows, block), bf16))
        + tuple(shape(v.shape, v.dtype) for v in (rhs, smoother, basis, tiles)),
        [hbm] * 4,
        [pltpu.SemaphoreType.DMA((4, cells))],
    )(*fixed)
    coarse, pivot = call(
        coarse_body,
        (shape((cells, size, size), bf16), shape((cells, 1, size), f32)),
        [vmem, vmem],
    )(tiles, basis)
    near = exchange(send, slabs, cols)
    near, coarse, pivot = lax.optimization_barrier((near, coarse, pivot))
    x_second, send = call(
        functools.partial(second_body, slab_cells),
        (shape((cells, rows, block), f32), shape((cells, rows, block), bf16)),
        [smem] + [vmem] * (4 + len(near)),
    )(neighbours, rhs, x_first, smoother, tiles, *near)
    near = exchange(send, slabs, cols)
    base, send = call(
        functools.partial(third_body, slab_cells),
        (shape((cells, rows, size), f32), shape((cells, 2 * rows, block), bf16)),
        [smem] + [vmem] * (5 + len(near)),
    )(neighbours, rhs, basis, coarse, pivot, tiles, *near)
    near = exchange(send, slabs, cols)
    return call(
        functools.partial(fourth_body, slab_cells),
        (shape((cells, rows, block), f32), shape((cells, rows, size), f32)),
        [smem] + [vmem] * (5 + len(near)),
    )(neighbours, base, x_second, basis, pivot, tiles, *near)


def solution(mesh):
    placed = (
        P(AXES, None, None),
        P(AXES, None, None, None),
        P(AXES, None),
        P(AXES, None, None),
        P(AXES, None, None),
    )
    return jax.shard_map(
        functools.partial(per_device, mesh.shape["slab"], mesh.shape["col"]),
        mesh=mesh,
        in_specs=placed,
        out_specs=(P(AXES, None, None), P(AXES, None, None)),
        check_vma=False,
    )
```

time: 89 us -> 76.9 us (0.86)
  blocking collectives: 31.9 us -> 43.7 us
  waiting for transfers between devices: 11.3 us -> 1.13 us
  starting transfers between devices: 28.2 us -> 22.6 us
  local copies, waits for them, and re-layouts: 4.96 us -> 0.01 us
  Pallas kernels: 11.5 us -> 8.5 us
    all_gather x6 -> x9, blocking collectives: 31.9 us -> 43.7 us  [the longest x6 25.6 us: gather(): lax.all_gather(values, AXES, axis=0, tiled=True, axis_index_groups=pairs(...]
    ppermute x3, waiting for transfers between devices: 11.3 us -> 1.13 us  [cross(): lax.ppermute(values, AXES, [(s * cols + c, target(s, c)) for s in range(s...]
    ppermute x3, starting transfers between devices: 28.2 us -> 22.6 us  [cross(): lax.ppermute(values, AXES, [(s * cols + c, target(s, c)) for s in range(s...]
    unnamed x14 -> x2, local copies, waits for them, and re-layouts: 4.96 us -> 0.01 us
    pallas_call x1 -> x2, Pallas kernels: 0.86 us -> 3.09 us  [the longest x1 2.33 us: per_device(): call(first_body, (shape((cells, rows, block), f32), shape((cells, rows, b...]
    pallas_call x1, Pallas kernels: 3.51 us -> 1.75 us  [per_device(): call(functools.partial(third_body, slab_cells), (shape((cells, rows, size...]
    pallas_call x1, Pallas kernels: 3.12 us -> 1.36 us  [per_device(): call(functools.partial(second_body, slab_cells), (shape((cells, rows, blo...]
    pallas_call x1, Pallas kernels: 3.99 us -> 2.3 us  [per_device(): call(functools.partial(fourth_body, slab_cells), (shape((cells, rows, blo...]
  transfers between devices with their start and end apart: 3 -> 3, of which waited for: 3 -> 2; matrix products, arithmetic and copies ran while one was open for 0% -> 0% of each run, Pallas kernels for 0% -> 1%
where the time goes in v2:
time: 76.9 us; the launch traced here: 76.6 us
  blocking collectives  43.7 us (57%)
  starting transfers between devices  22.6 us (29%)
  Pallas kernels  8.5 us (11%)
  waiting for transfers between devices  1.13 us (1%)
    all_gather x6, blocking collectives, gather(): lax.all_gather(values, AXES, axis=0, tiled=True, axis_index_groups=pairs(...  25.6 us
    ppermute x3, starting transfers between devices, cross(): lax.ppermute(values, AXES, [(s * cols + c, target(s, c)) for s in range(s...  22.6 us
    all_gather x3, blocking collectives, exchange(): return (own, lax.all_gather(beside, 'col', axis=0, tiled=True))  18.1 us
    pallas_call x1, Pallas kernels, per_device(): call(first_body, (shape((cells, rows, block), f32), shape((cells, rows, b...  2.33 us
    pallas_call x1, Pallas kernels, per_device(): call(functools.partial(fourth_body, slab_cells), (shape((cells, rows, blo...  2.3 us
    pallas_call x1, Pallas kernels, per_device(): call(functools.partial(third_body, slab_cells), (shape((cells, rows, size...  1.75 us
  transfers between devices with their start and end apart: 3, of which 2 were waited for; matrix products, arithmetic and copies ran while one was open for 0% of the time, Pallas kernels for 1%

profile of v2, /device:TPU:1, one launch (start us, length us, event | category | flops | bytes accessed | tf_op | source)
XLA Modules:
  0.0 76.6 jit_solution(15972111438361243680)
XLA Ops:
  0.6 2.3 %shard_map.68 = (f32[2,32,384]{2,1,0:T(8,128)S(1)}, bf16[2,32,384]{2,1,0:T(8,128)(2,1)S(1)}, f32[2,32,384]{2,1,0:T(8,128)S(1)}, bf16[2,384,384]{2,1,0:T(8,128)(2...) custom-call(bf16[2,384,384]{2,1,0:T(8,128)(2,1)} %refs_0_.1, f32[2,32,384]{2,1,0:T(8,128)} %refs_1_.1, ...), custom_call_target="tpu_custom_call" | custom-call | tf_op jit(solution)/shard_map/pallas_call | solution.py:194
  3.0 0.0 copy-start
  3.0 8.4 %all_gather.27 = bf16[4,32,384]{2,1,0:T(8,128)(2,1)S(1)} all-gather(bf16[2,32,384]{2,1,0:T(8,128)(2,1)S(1)} %get-tuple-element.20), channel_id=1, replica_groups={{0,1},{2,3},{4,5},{6,7},{8,9},{10,11},{12,13},{14,15},{16,17},{18,19},{..., dimensions={0}, use_global_device_ids=true | all-gather | bytes 147456 | tf_op jit(solution)/shard_map/all_gather | solution.py:42
  11.3 10.4 %collective-permute-start = (bf16[4,32,384]{2,1,0:T(8,128)(2,1)S(1)}, bf16[4,32,384]{2,1,0:T(8,128)(2,1)S(1)}, u32[]{:S(2)}, u32[]{:S(2)}) collective-permute-start(bf16[4,32,384]{2,1,0:T(8,128)(2,1)S(1)} %all_gather.27), channel_id=1, source_target_pairs={{0,6},{1,511},{2,4},{3,509},{4,2},{5,11},{6,0},{7,9},{8,14},{9,7},... | collective-permute-start | bytes 294920 | tf_op jit(solution)/shard_map/ppermute | solution.py:61
  21.8 0.8 shard_map.69
  22.5 4.1 %all_gather.28.refs_0_ = bf16[8,32,384]{2,1,0:T(8,128)(2,1)S(1)} all-gather(bf16[4,32,384]{2,1,0:T(8,128)(2,1)S(1)} %all_gather.27), channel_id=1, replica_groups={{0,2},{1,3},{4,6},{5,7},{8,10},{9,11},{12,14},{13,15},{16,18},{17,19},{..., dimensions={0}, use_global_device_ids=true | all-gather | bytes 294912 | tf_op jit(solution)/shard_map/all_gather | solution.py:42
  26.7 0.0 collective-permute-done
  26.7 5.2 %all_gather.29.refs_1_ = bf16[16,32,384]{2,1,0:T(8,128)(2,1)S(1)} all-gather(bf16[4,32,384]{2,1,0:T(8,128)(2,1)S(1)} %collective-permute-done), channel_id=1, replica_groups=mesh['slab'=128,'col'=4] {'col'}, dimensions={0}, use_global_device_ids=true | all-gather | bytes 491520 | tf_op jit(solution)/shard_map/all_gather | solution.py:72
  31.9 0.0 copy-done
  31.9 1.4 %shard_map.70 = (f32[2,32,384]{2,1,0:T(8,128)S(1)}, bf16[2,32,384]{2,1,0:T(8,128)(2,1)S(1)}) custom-call(s32[2,6]{1,0:T(2,128)S(1)} %copy-done, f32[2,32,384]{2,1,0:T(8,128)S(1)} %get-tuple-element.18.rhs, f32[2,32,384]{2,1,0:T(8,128)S(1)} %get-tuple-element.26.x_first, bf16[2,384,384]{2,1,0:T(8,128)(2,1)S(1)} %get-tuple-element.27.smoother, ...), custom_call_target="tpu_custom_call" | custom-call | tf_op jit(solution)/shard_map/pallas_call | solution.py:208
  33.3 1.9 %all_gather.30 = bf16[4,32,384]{2,1,0:T(8,128)(2,1)S(1)} all-gather(bf16[2,32,384]{2,1,0:T(8,128)(2,1)S(1)} %get-tuple-element.30), channel_id=1, replica_groups={{0,1},{2,3},{4,5},{6,7},{8,9},{10,11},{12,13},{14,15},{16,17},{18,19},{..., dimensions={0}, use_global_device_ids=true | all-gather | bytes 147456 | tf_op jit(solution)/shard_map/all_gather | solution.py:42
  35.1 5.6 %collective-permute-start.1 = (bf16[4,32,384]{2,1,0:T(8,128)(2,1)S(1)}, bf16[4,32,384]{2,1,0:T(8,128)(2,1)S(1)}, u32[]{:S(2)}, u32[]{:S(2)}) collective-permute-start(bf16[4,32,384]{2,1,0:T(8,128)(2,1)S(1)} %all_gather.30), channel_id=1, source_target_pairs={{0,6},{1,511},{2,4},{3,509},{4,2},{5,11},{6,0},{7,9},{8,14},{9,7},... | collective-permute-start | bytes 294920 | tf_op jit(solution)/shard_map/ppermute | solution.py:61
  40.8 4.1 %all_gather.31.refs_0_ = bf16[8,32,384]{2,1,0:T(8,128)(2,1)S(1)} all-gather(bf16[4,32,384]{2,1,0:T(8,128)(2,1)S(1)} %all_gather.30), channel_id=1, replica_groups={{0,2},{1,3},{4,6},{5,7},{8,10},{9,11},{12,14},{13,15},{16,18},{17,19},{..., dimensions={0}, use_global_device_ids=true | all-gather | bytes 294912 | tf_op jit(solution)/shard_map/all_gather | solution.py:42
  44.9 1.0 %collective-permute-done.1 = bf16[4,32,384]{2,1,0:T(8,128)(2,1)S(1)} collective-permute-done((bf16[4,32,384]{2,1,0:T(8,128)(2,1)S(1)}, bf16[4,32,384]{2,1,0:T(8,128)(2,1)S(1)}, u32[]{:S(2)}, u32[]{:S(2)}) %collective-permute-start.1) | collective-permute-done | bytes 98336 | tf_op jit(solution)/shard_map/ppermute | solution.py:61
  45.9 5.4 %all_gather.32.refs_1_ = bf16[16,32,384]{2,1,0:T(8,128)(2,1)S(1)} all-gather(bf16[4,32,384]{2,1,0:T(8,128)(2,1)S(1)} %collective-permute-done.1), channel_id=1, replica_groups=mesh['slab'=128,'col'=4] {'col'}, dimensions={0}, use_global_device_ids=true | all-gather | bytes 491520 | tf_op jit(solution)/shard_map/all_gather | solution.py:72
  51.3 1.7 %shard_map.71 = (f32[2,32,256]{2,1,0:T(8,128)S(1)}, bf16[2,64,384]{2,1,0:T(8,128)(2,1)S(1)}) custom-call(s32[2,6]{1,0:T(2,128)S(1)} %copy-done, f32[2,32,384]{2,1,0:T(8,128)S(1)} %get-tuple-element.18.rhs, bf16[2,256,384]{2,1,0:T(8,128)(2,1)S(1)} %get-tuple-element.19.basis, bf16[2,256,256]{2,1,0:T(8,128)(2,1)S(1)} %get-tuple-element.24.coarse, ...), custom_call_target="tpu_custom_call" | custom-call | tf_op jit(solution)/shard_map/pallas_call | solution.py:214
  53.0 1.9 %all_gather.33 = bf16[4,64,384]{2,1,0:T(8,128)(2,1)S(1)} all-gather(bf16[2,64,384]{2,1,0:T(8,128)(2,1)S(1)} %get-tuple-element.33), channel_id=1, replica_groups={{0,1},{2,3},{4,5},{6,7},{8,9},{10,11},{12,13},{14,15},{16,17},{18,19},{..., dimensions={0}, use_global_device_ids=true | all-gather | bytes 294912 | tf_op jit(solution)/shard_map/all_gather | solution.py:42
  55.0 6.5 %collective-permute-start.2 = (bf16[4,64,384]{2,1,0:T(8,128)(2,1)S(1)}, bf16[4,64,384]{2,1,0:T(8,128)(2,1)S(1)}, u32[]{:S(2)}, u32[]{:S(2)}) collective-permute-start(bf16[4,64,384]{2,1,0:T(8,128)(2,1)S(1)} %all_gather.33), channel_id=1, source_target_pairs={{0,6},{1,511},{2,4},{3,509},{4,2},{5,11},{6,0},{7,9},{8,14},{9,7},... | collective-permute-start | bytes 589832 | tf_op jit(solution)/shard_map/ppermute | solution.py:61
  61.5 5.2 %all_gather.34.refs_0_ = bf16[8,64,384]{2,1,0:T(8,128)(2,1)S(1)} all-gather(bf16[4,64,384]{2,1,0:T(8,128)(2,1)S(1)} %all_gather.33), channel_id=1, replica_groups={{0,2},{1,3},{4,6},{5,7},{8,10},{9,11},{12,14},{13,15},{16,18},{17,19},{..., dimensions={0}, use_global_device_ids=true | all-gather | bytes 589824 | tf_op jit(solution)/shard_map/all_gather | solution.py:42
  66.7 0.1 collective-permute-done.2
  66.8 7.5 %all_gather.35.refs_1_ = bf16[16,64,384]{2,1,0:T(8,128)(2,1)S(1)} all-gather(bf16[4,64,384]{2,1,0:T(8,128)(2,1)S(1)} %collective-permute-done.2), channel_id=1, replica_groups=mesh['slab'=128,'col'=4] {'col'}, dimensions={0}, use_global_device_ids=true | all-gather | bytes 983040 | tf_op jit(solution)/shard_map/all_gather | solution.py:72
  74.3 2.3 %shard_map.72 = (f32[2,32,384]{2,1,0:T(8,128)}, f32[2,32,256]{2,1,0:T(8,128)}) custom-call(s32[2,6]{1,0:T(2,128)S(1)} %copy-done, f32[2,32,256]{2,1,0:T(8,128)S(1)} %get-tuple-element.31.base, f32[2,32,384]{2,1,0:T(8,128)S(1)} %get-tuple-element.32.x_second, bf16[2,256,384]{2,1,0:T(8,128)(2,1)S(1)} %get-tuple-element.19.basis, ...), custom_call_target="tpu_custom_call" | custom-call | tf_op jit(solution)/shard_map/pallas_call | solution.py:220
Async XLA Ops:
  3.0 28.9 %copy-start = (s32[2,6]{1,0:T(2,128)S(1)}, s32[2,6]{1,0:T(2,128)}, u32[]{:S(2)}) copy-start(s32[2,6]{1,0:T(2,128)} %nb.5) | copy-start | bytes 148
  11.3 15.3 %collective-permute-start = (bf16[4,32,384]{2,1,0:T(8,128)(2,1)S(1)}, bf16[4,32,384]{2,1,0:T(8,128)(2,1)S(1)}, u32[]{:S(2)}, u32[]{:S(2)}) collective-permute-start(bf16[4,32,384]{2,1,0:T(8,128)(2,1)S(1)} %all_gather.27), channel_id=1, source_target_pairs={{0,6},{1,511},{2,4},{3,509},{4,2},{5,11},{6,0},{7,9},{8,14},{9,7},... | collective-permute-start | bytes 294920 | tf_op jit(solution)/shard_map/ppermute | solution.py:61
  35.1 10.8 %collective-permute-start.1 = (bf16[4,32,384]{2,1,0:T(8,128)(2,1)S(1)}, bf16[4,32,384]{2,1,0:T(8,128)(2,1)S(1)}, u32[]{:S(2)}, u32[]{:S(2)}) collective-permute-start(bf16[4,32,384]{2,1,0:T(8,128)(2,1)S(1)} %all_gather.30), channel_id=1, source_target_pairs={{0,6},{1,511},{2,4},{3,509},{4,2},{5,11},{6,0},{7,9},{8,14},{9,7},... | collective-permute-start | bytes 294920 | tf_op jit(solution)/shard_map/ppermute | solution.py:61
  55.0 11.8 %collective-permute-start.2 = (bf16[4,64,384]{2,1,0:T(8,128)(2,1)S(1)}, bf16[4,64,384]{2,1,0:T(8,128)(2,1)S(1)}, u32[]{:S(2)}, u32[]{:S(2)}) collective-permute-start(bf16[4,64,384]{2,1,0:T(8,128)(2,1)S(1)} %all_gather.33), channel_id=1, source_target_pairs={{0,6},{1,511},{2,4},{3,509},{4,2},{5,11},{6,0},{7,9},{8,14},{9,7},... | collective-permute-start | bytes 589832 | tf_op jit(solution)/shard_map/ppermute | solution.py:61

commit v3 on v2

--- a/solution.py
+++ b/solution.py
@@ -65,20 +65,60 @@
     )
 
 
-def exchange(cells, slabs, cols):
+def cross_now(values, slabs, cols):
+    return lax.all_gather(
+        values,
+        AXES,
+        axis=0,
+        tiled=True,
+        axis_index_groups=pairs(slabs, cols, lambda s, c: crossing(s, c, slabs)),
+    )
+
+
+def merge_body(slabs, cells, beside, out):
+    n, extra = cells.shape[0], out.shape[0] - cells.shape[0]
+    first = 0
+    if beside.shape[0] != extra:
+        s, c = lax.axis_index("slab"), lax.axis_index("col")
+        up = lax.rem(s, 2) == lax.rem(c, 2)
+        other = lax.rem(jnp.where(up, s + 1, s - 1 + slabs), slabs)
+        first = jnp.where(s < other, extra, 0)
+    for i in range(n):
+        out[i] = cells[i]
+    for i in range(extra):
+        out[n + i] = beside[first + i]
+
+
+def joined_exchange(cells, slabs, cols, move):
+    chip = gather(cells, slabs, cols, 1)
+    beside = move(chip, slabs, cols)
+    total = (cells.shape[0] + chip.shape[0],) + cells.shape[1:]
+    (joined,) = call(
+        functools.partial(merge_body, slabs),
+        (jax.ShapeDtypeStruct(total, cells.dtype),),
+        [pl.BlockSpec(memory_space=VMEM)] * 2,
+    )(cells, beside)
+    return (lax.all_gather(joined, "col", axis=0, tiled=True),)
+
+
+def exchange_apart(cells, slabs, cols):
     chip = gather(cells, slabs, cols, 1)
     beside = cross(chip, slabs, cols)
     own = gather(chip, slabs, cols, 2)
     return own, lax.all_gather(beside, "col", axis=0, tiled=True)
 
 
-def pick(near, cell, here, slab_cells):
+def pick(near, cell, here, slab_cells, cells):
     slab = lax.div(cell, slab_cells)
     offset = lax.rem(cell, slab_cells)
     half = slab_cells // 2
     chip, inner = lax.div(offset, half), lax.rem(offset, half)
     odd = jnp.where(lax.div(slab, 2) == lax.div(here, 2), 0, 1)
     col = 2 * (1 - chip) + odd
+    if len(near) == 1:
+        stride = half + cells
+        mine = lax.div(offset, cells) * stride + lax.rem(offset, cells)
+        return near[0][jnp.where(slab == here, mine, col * stride + cells + inner)]
     own, halo = near
     return jnp.where(slab == here, own[offset], halo[col * half + inner])
 
@@ -89,41 +129,65 @@
     sums = [None] * cells
     for t in range(first, kinds):
         for g in range(cells):
-            part = dot(pick(near, nb[g, t], here, slab_cells), tiles[g, t])
+            part = dot(pick(near, nb[g, t], here, slab_cells, cells), tiles[g, t])
             sums[g] = part if sums[g] is None else sums[g] + part
     return sums
 
 
-def first_body(*refs):
-    sources, (x_out, xb_out, rhs, smoother, basis, tiles), sems = refs[:4], refs[4:10], refs[10]
+def load(source, target, sems):
     copies = []
-    for k, (source, target) in enumerate(zip(sources, (smoother, rhs, tiles, basis))):
-        for g in range(rhs.shape[0]):
-            copy = pltpu.make_async_copy(source.at[g], target.at[g], sems.at[k, g])
-            copy.start()
-            copies.append(copy)
-    for copy in copies[: 2 * rhs.shape[0]]:
-        copy.wait()
-    for g in range(rhs.shape[0]):
+    for g in range(target.shape[0]):
+        copies.append(pltpu.make_async_copy(source.at[g], target.at[g], sems.at[g]))
+        copies[-1].start()
+    return copies
+
+
+def first_body(smoother_hbm, rhs_hbm, x_out, xb_out, smoother, rhs, smoother_sems, rhs_sems):
+    copies = zip(
+        load(smoother_hbm, smoother, smoother_sems), load(rhs_hbm, rhs, rhs_sems)
+    )
+    for g, pair in enumerate(copies):
+        for copy in pair:
+            copy.wait()
         x = dot(rhs[g].astype(bf16), smoother[g])
         x_out[g] = x
         xb_out[g] = x.astype(bf16)
-    for copy in copies[2 * rhs.shape[0] :]:
-        copy.wait()
-
-
-def coarse_body(own_tiles, basis, coarse_out, pivot_out):
+
+
+def coarse_body(
+    tiles_hbm, basis_hbm, tiles, basis, coarse_out, pivot_out, own_sems, basis_sems, rest_sems
+):
+    cells, kinds = tiles.shape[0], tiles.shape[1]
+    basis_copies = load(basis_hbm, basis, basis_sems)
+    parts = [
+        [
+            pltpu.make_async_copy(
+                tiles_hbm.at[g, pl.ds(first, count)],
+                tiles.at[g, pl.ds(first, count)],
+                sems.at[g],
+            )
+            for g in range(cells)
+        ]
+        for first, count, sems in ((0, 1, own_sems), (1, kinds - 1, rest_sems))
+    ]
+    for part in parts:
+        for copy in part:
+            copy.start()
     size = basis.shape[1]
     eye = lax.broadcasted_iota(jnp.int32, (size, size), 0) == lax.broadcasted_iota(
         jnp.int32, (size, size), 1
     )
-    for g in range(basis.shape[0]):
-        upper = dot(basis[g], own_tiles[g, 0]).astype(bf16)
+    for g in range(cells):
+        basis_copies[g].wait()
+        parts[0][g].wait()
+        upper = dot(basis[g], tiles[g, 0]).astype(bf16)
         coarse = dot_t(upper, basis[g]).astype(bf16)
         coarse_out[g] = coarse
         pivot_out[g] = jnp.sum(
             jnp.where(eye, coarse.astype(f32), 0.0), axis=0, keepdims=True
         )
+    for copy in parts[1]:
+        copy.wait()
 
 
 def second_body(slab_cells, nb, rhs, x_first, smoother, tiles, *refs):
@@ -191,32 +255,42 @@
     fixed = [
         pltpu.with_memory_space_constraint(v, pltpu.HBM) for v in (smoother, rhs, tiles, basis)
     ]
-    x_first, send, rhs, smoother, basis, tiles = call(
+    sems = pltpu.SemaphoreType.DMA((cells,))
+    x_first, send, smoother, rhs = call(
         first_body,
-        (shape((cells, rows, block), f32), shape((cells, rows, block), bf16))
-        + tuple(shape(v.shape, v.dtype) for v in (rhs, smoother, basis, tiles)),
-        [hbm] * 4,
-        [pltpu.SemaphoreType.DMA((4, cells))],
-    )(*fixed)
-    coarse, pivot = call(
+        (
+            shape((cells, rows, block), f32),
+            shape((cells, rows, block), bf16),
+            shape(smoother.shape, bf16),
+            shape(rhs.shape, f32),
+        ),
+        [hbm] * 2,
+        [sems] * 2,
+    )(*fixed[:2])
+    tiles, basis, coarse, pivot = call(
         coarse_body,
-        (shape((cells, size, size), bf16), shape((cells, 1, size), f32)),
-        [vmem, vmem],
-    )(tiles, basis)
-    near = exchange(send, slabs, cols)
-    near, coarse, pivot = lax.optimization_barrier((near, coarse, pivot))
+        (
+            shape(tiles.shape, bf16),
+            shape(basis.shape, bf16),
+            shape((cells, size, size), bf16),
+            shape((cells, 1, size), f32),
+        ),
+        [hbm] * 2,
+        [sems] * 3,
+    )(*fixed[2:])
+    near = joined_exchange(send, slabs, cols, cross)
     x_second, send = call(
         functools.partial(second_body, slab_cells),
         (shape((cells, rows, block), f32), shape((cells, rows, block), bf16)),
         [smem] + [vmem] * (4 + len(near)),
     )(neighbours, rhs, x_first, smoother, tiles, *near)
-    near = exchange(send, slabs, cols)
+    near = joined_exchange(send, slabs, cols, cross_now)
     base, send = call(
         functools.partial(third_body, slab_cells),
         (shape((cells, rows, size), f32), shape((cells, 2 * rows, block), bf16)),
         [smem] + [vmem] * (5 + len(near)),
     )(neighbours, rhs, basis, coarse, pivot, tiles, *near)
-    near = exchange(send, slabs, cols)
+    near = exchange_apart(send, slabs, cols)
     return call(
         functools.partial(fourth_body, slab_cells),
         (shape((cells, rows, block), f32), shape((cells, rows, size), f32)),

time: 76.9 us -> 76.4 us (level)
  blocking collectives: 43.7 us -> 47.8 us
  starting transfers between devices: 22.6 us -> 18.7 us
  waiting for transfers between devices: 1.13 us -> 0.01 us
    all_gather x3 -> x4, blocking collectives: 18.1 us -> 30.4 us  [the longest x2 13.5 us: joined_exchange(): return (lax.all_gather(joined, 'col', axis=0, tiled=True),)]
    all_gather x6 -> x4, blocking collectives: 25.6 us -> 17.4 us  [gather(): lax.all_gather(values, AXES, axis=0, tiled=True, axis_index_groups=pairs(...]
    ppermute x3 -> x2, starting transfers between devices: 22.6 us -> 18.7 us  [cross(): lax.ppermute(values, AXES, [(s * cols + c, target(s, c)) for s in range(s...]
    pallas_call x1 -> x3, Pallas kernels: 0.76 us -> 2.21 us  [the longest x1 2.18 us: per_device(): call(coarse_body, (shape(tiles.shape, bf16), shape(basis.shape, bf16), sh...]
    ppermute x3 -> x2, waiting for transfers between devices: 1.13 us -> 0.01 us  [cross(): lax.ppermute(values, AXES, [(s * cols + c, target(s, c)) for s in range(s...]
    pallas_call x1, Pallas kernels: 2.33 us -> 1.36 us  [per_device(): call(first_body, (shape((cells, rows, block), f32), shape((cells, rows, b...]
  transfers between devices with their start and end apart: 3 -> 2, of which waited for: 2 -> 0; matrix products, arithmetic and copies ran while one was open for 0% -> 0% of each run, Pallas kernels for 1% -> 3%
where the time goes in v3:
time: 76.4 us; the launch traced here: 76.2 us
  blocking collectives  47.8 us (63%)
  starting transfers between devices  18.7 us (24%)
  Pallas kernels  8.97 us (12%)
    ppermute x2, starting transfers between devices, cross(): lax.ppermute(values, AXES, [(s * cols + c, target(s, c)) for s in range(s...  18.7 us
    all_gather x4, blocking collectives, gather(): lax.all_gather(values, AXES, axis=0, tiled=True, axis_index_groups=pairs(...  17.4 us
    all_gather x2, blocking collectives, joined_exchange(): return (lax.all_gather(joined, 'col', axis=0, tiled=True),)  13.5 us
    all_gather x1, blocking collectives, cross_now(): lax.all_gather(values, AXES, axis=0, tiled=True, axis_index_groups=pairs(...  9.55 us
    all_gather x1, blocking collectives, exchange_apart(): return (own, lax.all_gather(beside, 'col', axis=0, tiled=True))  7.37 us
    pallas_call x1, Pallas kernels, per_device(): call(functools.partial(fourth_body, slab_cells), (shape((cells, rows, blo...  2.3 us
    pallas_call x1, Pallas kernels, per_device(): call(coarse_body, (shape(tiles.shape, bf16), shape(basis.shape, bf16), sh...  2.18 us
    pallas_call x1, Pallas kernels, per_device(): call(functools.partial(third_body, slab_cells), (shape((cells, rows, size...  1.75 us
  transfers between devices with their start and end apart: 2, of which 0 were waited for; matrix products, arithmetic and copies ran while one was open for 0% of the time, Pallas kernels for 3%

profile of v3, /device:TPU:1, one launch (start us, length us, event | category | flops | bytes accessed | tf_op | source)
XLA Modules:
  0.0 76.2 jit_solution(7431865003804988400)
XLA Ops:
  0.6 0.0 copy-start
  0.6 1.4 %shard_map.68 = (f32[2,32,384]{2,1,0:T(8,128)S(1)}, bf16[2,32,384]{2,1,0:T(8,128)(2,1)S(1)}, bf16[2,384,384]{2,1,0:T(8,128)(2,1)S(1)}, f32[2,32,384]{2,1,0:T(8,128)S(1)}) custom-call(bf16[2,384,384]{2,1,0:T(8,128)(2,1)} %smoother_hbm.1, f32[2,32,384]{2,1,0:T(8,128)} %rhs_hbm.1), custom_call_target="tpu_custom_call" | custom-call | tf_op jit(solution)/shard_map/pallas_call | solution.py:259
  2.0 8.4 %all_gather.24 = bf16[4,32,384]{2,1,0:T(8,128)(2,1)S(1)} all-gather(bf16[2,32,384]{2,1,0:T(8,128)(2,1)S(1)} %get-tuple-element.21.cells), channel_id=1, replica_groups={{0,1},{2,3},{4,5},{6,7},{8,9},{10,11},{12,13},{14,15},{16,17},{18,19},{..., dimensions={0}, use_global_device_ids=true | all-gather | bytes 147456 | tf_op jit(solution)/shard_map/all_gather | solution.py:42
  10.4 10.4 %collective-permute-start = (bf16[4,32,384]{2,1,0:T(8,128)(2,1)S(1)}, bf16[4,32,384]{2,1,0:T(8,128)(2,1)S(1)}, u32[]{:S(2)}, u32[]{:S(2)}) collective-permute-start(bf16[4,32,384]{2,1,0:T(8,128)(2,1)S(1)} %all_gather.24), channel_id=1, source_target_pairs={{0,6},{1,511},{2,4},{3,509},{4,2},{5,11},{6,0},{7,9},{8,14},{9,7},... | collective-permute-start | bytes 294920 | tf_op jit(solution)/shard_map/ppermute | solution.py:61
  20.8 2.2 %shard_map.69 = (bf16[2,6,384,384]{3,2,1,0:T(8,128)(2,1)S(1)}, bf16[2,256,384]{2,1,0:T(8,128)(2,1)S(1)}, bf16[2,256,256]{2,1,0:T(8,128)(2,1)S(1)}, f32[2,1,256]{2,1,0:T(1,128)S(1)}) custom-call(bf16[2,6,384,384]{3,2,1,0:T(8,128)(2,1)} %tiles_hbm.1, bf16[2,256,384]{2,1,0:T(8,128)(2,1)} %basis_hbm.1), custom_call_target="tpu_custom_call" | custom-call | tf_op jit(solution)/shard_map/pallas_call | solution.py:270
  23.0 0.0 collective-permute-done.beside
  23.0 6.2 %all_gather.25.refs_0_ = bf16[24,32,384]{2,1,0:T(8,128)(2,1)S(1)} all-gather(bf16[6,32,384]{2,1,0:T(8,128)(2,1)S(1)} %shard_map.70), channel_id=1, replica_groups=mesh['slab'=128,'col'=4] {'col'}, dimensions={0}, use_global_device_ids=true | all-gather | bytes 737280 | tf_op jit(solution)/shard_map/all_gather | solution.py:101
  29.2 0.0 copy-done
  29.2 1.4 %shard_map.71 = (f32[2,32,384]{2,1,0:T(8,128)S(1)}, bf16[2,32,384]{2,1,0:T(8,128)(2,1)S(1)}) custom-call(s32[2,6]{1,0:T(2,128)S(1)} %copy-done, f32[2,32,384]{2,1,0:T(8,128)S(1)} %get-tuple-element.14.rhs, f32[2,32,384]{2,1,0:T(8,128)S(1)} %get-tuple-element.19.x_first, bf16[2,384,384]{2,1,0:T(8,128)(2,1)S(1)} %get-tuple-element.20.smoother, ...), custom_call_target="tpu_custom_call" | custom-call | tf_op jit(solution)/shard_map/pallas_call | solution.py:282
  30.6 1.9 %all_gather.26 = bf16[4,32,384]{2,1,0:T(8,128)(2,1)S(1)} all-gather(bf16[2,32,384]{2,1,0:T(8,128)(2,1)S(1)} %get-tuple-element.22.cells), channel_id=1, replica_groups={{0,1},{2,3},{4,5},{6,7},{8,9},{10,11},{12,13},{14,15},{16,17},{18,19},{..., dimensions={0}, use_global_device_ids=true | all-gather | bytes 147456 | tf_op jit(solution)/shard_map/all_gather | solution.py:42
  32.4 9.5 %all_gather.27.beside = bf16[8,32,384]{2,1,0:T(8,128)(2,1)S(1)} all-gather(bf16[4,32,384]{2,1,0:T(8,128)(2,1)S(1)} %all_gather.26), channel_id=1, replica_groups={{0,6},{1,511},{2,4},{3,509},{5,11},{7,9},{8,14},{10,12},{13,19},{15,17}..., dimensions={0}, use_global_device_ids=true | all-gather | bytes 294912 | tf_op jit(solution)/shard_map/all_gather | solution.py:69
  42.0 7.3 %all_gather.28.refs_0_ = bf16[24,32,384]{2,1,0:T(8,128)(2,1)S(1)} all-gather(bf16[6,32,384]{2,1,0:T(8,128)(2,1)S(1)} %shard_map.72), channel_id=1, replica_groups=mesh['slab'=128,'col'=4] {'col'}, dimensions={0}, use_global_device_ids=true | all-gather | bytes 737280 | tf_op jit(solution)/shard_map/all_gather | solution.py:101
  49.3 1.7 %shard_map.73 = (f32[2,32,256]{2,1,0:T(8,128)S(1)}, bf16[2,64,384]{2,1,0:T(8,128)(2,1)S(1)}) custom-call(s32[2,6]{1,0:T(2,128)S(1)} %copy-done, f32[2,32,384]{2,1,0:T(8,128)S(1)} %get-tuple-element.14.rhs, bf16[2,256,384]{2,1,0:T(8,128)(2,1)S(1)} %get-tuple-element.15.basis, bf16[2,256,256]{2,1,0:T(8,128)(2,1)S(1)} %get-tuple-element.16.coarse, ...), custom_call_target="tpu_custom_call" | custom-call | tf_op jit(solution)/shard_map/pallas_call | solution.py:288
  51.1 1.9 %all_gather.29 = bf16[4,64,384]{2,1,0:T(8,128)(2,1)S(1)} all-gather(bf16[2,64,384]{2,1,0:T(8,128)(2,1)S(1)} %get-tuple-element.25), channel_id=1, replica_groups={{0,1},{2,3},{4,5},{6,7},{8,9},{10,11},{12,13},{14,15},{16,17},{18,19},{..., dimensions={0}, use_global_device_ids=true | all-gather | bytes 294912 | tf_op jit(solution)/shard_map/all_gather | solution.py:42
  53.0 8.3 %collective-permute-start.1 = (bf16[4,64,384]{2,1,0:T(8,128)(2,1)S(1)}, bf16[4,64,384]{2,1,0:T(8,128)(2,1)S(1)}, u32[]{:S(2)}, u32[]{:S(2)}) collective-permute-start(bf16[4,64,384]{2,1,0:T(8,128)(2,1)S(1)} %all_gather.29), channel_id=1, source_target_pairs={{0,6},{1,511},{2,4},{3,509},{4,2},{5,11},{6,0},{7,9},{8,14},{9,7},... | collective-permute-start | bytes 589832 | tf_op jit(solution)/shard_map/ppermute | solution.py:61
  61.3 5.2 %all_gather.30.refs_0_ = bf16[8,64,384]{2,1,0:T(8,128)(2,1)S(1)} all-gather(bf16[4,64,384]{2,1,0:T(8,128)(2,1)S(1)} %all_gather.29), channel_id=1, replica_groups={{0,2},{1,3},{4,6},{5,7},{8,10},{9,11},{12,14},{13,15},{16,18},{17,19},{..., dimensions={0}, use_global_device_ids=true | all-gather | bytes 589824 | tf_op jit(solution)/shard_map/all_gather | solution.py:42
  66.5 0.0 collective-permute-done.1
  66.5 7.4 %all_gather.31.refs_1_ = bf16[16,64,384]{2,1,0:T(8,128)(2,1)S(1)} all-gather(bf16[4,64,384]{2,1,0:T(8,128)(2,1)S(1)} %collective-permute-done.1), channel_id=1, replica_groups=mesh['slab'=128,'col'=4] {'col'}, dimensions={0}, use_global_device_ids=true | all-gather | bytes 983040 | tf_op jit(solution)/shard_map/all_gather | solution.py:108
  73.9 2.3 %shard_map.74 = (f32[2,32,384]{2,1,0:T(8,128)}, f32[2,32,256]{2,1,0:T(8,128)}) custom-call(s32[2,6]{1,0:T(2,128)S(1)} %copy-done, f32[2,32,256]{2,1,0:T(8,128)S(1)} %get-tuple-element.23.base, f32[2,32,384]{2,1,0:T(8,128)S(1)} %get-tuple-element.24.x_second, bf16[2,256,384]{2,1,0:T(8,128)(2,1)S(1)} %get-tuple-element.15.basis, ...), custom_call_target="tpu_custom_call" | custom-call | tf_op jit(solution)/shard_map/pallas_call | solution.py:294
  (2 shorter events, 0.0 us)
Async XLA Ops:
  0.6 28.6 %copy-start = (s32[2,6]{1,0:T(2,128)S(1)}, s32[2,6]{1,0:T(2,128)}, u32[]{:S(2)}) copy-start(s32[2,6]{1,0:T(2,128)} %nb.5) | copy-start | bytes 148
  10.4 12.6 %collective-permute-start = (bf16[4,32,384]{2,1,0:T(8,128)(2,1)S(1)}, bf16[4,32,384]{2,1,0:T(8,128)(2,1)S(1)}, u32[]{:S(2)}, u32[]{:S(2)}) collective-permute-start(bf16[4,32,384]{2,1,0:T(8,128)(2,1)S(1)} %all_gather.24), channel_id=1, source_target_pairs={{0,6},{1,511},{2,4},{3,509},{4,2},{5,11},{6,0},{7,9},{8,14},{9,7},... | collective-permute-start | bytes 294920 | tf_op jit(solution)/shard_map/ppermute | solution.py:61
  53.0 13.5 %collective-permute-start.1 = (bf16[4,64,384]{2,1,0:T(8,128)(2,1)S(1)}, bf16[4,64,384]{2,1,0:T(8,128)(2,1)S(1)}, u32[]{:S(2)}, u32[]{:S(2)}) collective-permute-start(bf16[4,64,384]{2,1,0:T(8,128)(2,1)S(1)} %all_gather.29), channel_id=1, source_target_pairs={{0,6},{1,511},{2,4},{3,509},{4,2},{5,11},{6,0},{7,9},{8,14},{9,7},... | collective-permute-start | bytes 589832 | tf_op jit(solution)/shard_map/ppermute | solution.py:61

commit v4 on v3

--- a/solution.py
+++ b/solution.py
@@ -193,8 +193,11 @@
 def second_body(slab_cells, nb, rhs, x_first, smoother, tiles, *refs):
     *near, x_out, xb_out = refs
     sums = apply_tiles(near, nb, tiles, slab_cells)
-    for g, image in enumerate(sums):
-        x = x_first[g] + dot((rhs[g] - image).astype(bf16), smoother[g])
+    steps = [
+        dot((rhs[g] - image).astype(bf16), smoother[g]) for g, image in enumerate(sums)
+    ]
+    for g, step in enumerate(steps):
+        x = x_first[g] + step
         x_out[g] = x
         xb_out[g] = x.astype(bf16)
 
@@ -205,15 +208,17 @@
     *near, base_out, fine_out = refs
     sums = apply_tiles(near, nb, tiles, slab_cells)
     rows = rhs.shape[1]
-    for g, image in enumerate(sums):
-        coarse_rhs = dot_t((rhs[g] - image).astype(bf16), basis[g])
-        c_first = damping * coarse_rhs / pivot[g]
-        rounded = c_first.astype(bf16)
-        own = dot(rounded, coarse[g])
-        base_out[g] = c_first + damping * (coarse_rhs - own) / pivot[g]
-        high, low = split(dot(rounded, basis[g]))
+    every = range(len(sums))
+    coarse_rhs = [dot_t((rhs[g] - sums[g]).astype(bf16), basis[g]) for g in every]
+    c_first = [damping * coarse_rhs[g] / pivot[g] for g in every]
+    rounded = [c.astype(bf16) for c in c_first]
+    fine = [dot(rounded[g], basis[g]) for g in every]
+    own = [dot(rounded[g], coarse[g]) for g in every]
+    for g in every:
+        high, low = split(fine[g])
         fine_out[g, :rows] = high
         fine_out[g, rows:] = low
+        base_out[g] = c_first[g] + damping * (coarse_rhs[g] - own[g]) / pivot[g]
 
 
 def fourth_body(
@@ -222,13 +227,14 @@
     *near, sol_out, iter_out = refs
     sums = apply_tiles(near, nb, tiles, slab_cells, 1)
     rows = x_second.shape[1]
-    for g, image in enumerate(sums):
-        parts = jnp.concatenate(split(image[:rows] + image[rows:]))
-        both = dot_t(parts, basis[g])
-        rest = both[:rows] + both[rows:]
-        iterate = base[g] - damping * rest / pivot[g]
-        iter_out[g] = iterate
-        sol_out[g] = x_second[g] + dot(iterate.astype(bf16), basis[g])
+    every = range(len(sums))
+    parts = [jnp.concatenate(split(sums[g][:rows] + sums[g][rows:])) for g in every]
+    both = [dot_t(parts[g], basis[g]) for g in every]
+    iterates = [base[g] - damping * (both[g][:rows] + both[g][rows:]) / pivot[g] for g in every]
+    steps = [dot(iterates[g].astype(bf16), basis[g]) for g in every]
+    for g in every:
+        iter_out[g] = iterates[g]
+        sol_out[g] = x_second[g] + steps[g]
 
 
 def call(body, outs, specs, scratch=(), limit=24 * 2**20, moved=None):

time: 76.4 us -> 76 us (level)
  no operation moved by 1% of the time
where the time goes in v4:
time: 76 us; the launch traced here: 75.7 us
  blocking collectives  47.8 us (63%)
  starting transfers between devices  18.7 us (25%)
  Pallas kernels  8.53 us (11%)
    ppermute x2, starting transfers between devices, cross(): lax.ppermute(values, AXES, [(s * cols + c, target(s, c)) for s in range(s...  18.7 us
    all_gather x4, blocking collectives, gather(): lax.all_gather(values, AXES, axis=0, tiled=True, axis_index_groups=pairs(...  17.4 us
    all_gather x2, blocking collectives, joined_exchange(): return (lax.all_gather(joined, 'col', axis=0, tiled=True),)  13.5 us
    all_gather x1, blocking collectives, cross_now(): lax.all_gather(values, AXES, axis=0, tiled=True, axis_index_groups=pairs(...  9.55 us
    all_gather x1, blocking collectives, exchange_apart(): return (own, lax.all_gather(beside, 'col', axis=0, tiled=True))  7.37 us
    pallas_call x1, Pallas kernels, per_device(): call(coarse_body, (shape(tiles.shape, bf16), shape(basis.shape, bf16), sh...  2.18 us
    pallas_call x1, Pallas kernels, per_device(): call(functools.partial(fourth_body, slab_cells), (shape((cells, rows, blo...  2.09 us
  transfers between devices with their start and end apart: 2, of which 0 were waited for; matrix products, arithmetic and copies ran while one was open for 0% of the time, Pallas kernels for 3%

profile of v4, /device:TPU:1, one launch (start us, length us, event | category | flops | bytes accessed | tf_op | source)
XLA Modules:
  0.0 75.7 jit_solution(15070101350485694921)
XLA Ops:
  0.6 0.0 copy-start
  0.6 1.4 %shard_map.68 = (f32[2,32,384]{2,1,0:T(8,128)S(1)}, bf16[2,32,384]{2,1,0:T(8,128)(2,1)S(1)}, bf16[2,384,384]{2,1,0:T(8,128)(2,1)S(1)}, f32[2,32,384]{2,1,0:T(8,128)S(1)}) custom-call(bf16[2,384,384]{2,1,0:T(8,128)(2,1)} %smoother_hbm.1, f32[2,32,384]{2,1,0:T(8,128)} %rhs_hbm.1), custom_call_target="tpu_custom_call" | custom-call | tf_op jit(solution)/shard_map/pallas_call | solution.py:265
  2.0 8.4 %all_gather.24 = bf16[4,32,384]{2,1,0:T(8,128)(2,1)S(1)} all-gather(bf16[2,32,384]{2,1,0:T(8,128)(2,1)S(1)} %get-tuple-element.21.cells), channel_id=1, replica_groups={{0,1},{2,3},{4,5},{6,7},{8,9},{10,11},{12,13},{14,15},{16,17},{18,19},{..., dimensions={0}, use_global_device_ids=true | all-gather | bytes 147456 | tf_op jit(solution)/shard_map/all_gather | solution.py:42
  10.4 10.4 %collective-permute-start = (bf16[4,32,384]{2,1,0:T(8,128)(2,1)S(1)}, bf16[4,32,384]{2,1,0:T(8,128)(2,1)S(1)}, u32[]{:S(2)}, u32[]{:S(2)}) collective-permute-start(bf16[4,32,384]{2,1,0:T(8,128)(2,1)S(1)} %all_gather.24), channel_id=1, source_target_pairs={{0,6},{1,511},{2,4},{3,509},{4,2},{5,11},{6,0},{7,9},{8,14},{9,7},... | collective-permute-start | bytes 294920 | tf_op jit(solution)/shard_map/ppermute | solution.py:61
  20.8 2.2 %shard_map.69 = (bf16[2,6,384,384]{3,2,1,0:T(8,128)(2,1)S(1)}, bf16[2,256,384]{2,1,0:T(8,128)(2,1)S(1)}, bf16[2,256,256]{2,1,0:T(8,128)(2,1)S(1)}, f32[2,1,256]{2,1,0:T(1,128)S(1)}) custom-call(bf16[2,6,384,384]{3,2,1,0:T(8,128)(2,1)} %tiles_hbm.1, bf16[2,256,384]{2,1,0:T(8,128)(2,1)} %basis_hbm.1), custom_call_target="tpu_custom_call" | custom-call | tf_op jit(solution)/shard_map/pallas_call | solution.py:276
  23.0 0.0 collective-permute-done.beside
  23.0 6.2 %all_gather.25.refs_0_ = bf16[24,32,384]{2,1,0:T(8,128)(2,1)S(1)} all-gather(bf16[6,32,384]{2,1,0:T(8,128)(2,1)S(1)} %shard_map.70), channel_id=1, replica_groups=mesh['slab'=128,'col'=4] {'col'}, dimensions={0}, use_global_device_ids=true | all-gather | bytes 737280 | tf_op jit(solution)/shard_map/all_gather | solution.py:101
  29.2 0.0 copy-done
  29.2 1.4 %shard_map.71 = (f32[2,32,384]{2,1,0:T(8,128)S(1)}, bf16[2,32,384]{2,1,0:T(8,128)(2,1)S(1)}) custom-call(s32[2,6]{1,0:T(2,128)S(1)} %copy-done, f32[2,32,384]{2,1,0:T(8,128)S(1)} %get-tuple-element.14.rhs, f32[2,32,384]{2,1,0:T(8,128)S(1)} %get-tuple-element.19.x_first, bf16[2,384,384]{2,1,0:T(8,128)(2,1)S(1)} %get-tuple-element.20.smoother, ...), custom_call_target="tpu_custom_call" | custom-call | tf_op jit(solution)/shard_map/pallas_call | solution.py:288
  30.6 1.9 %all_gather.26 = bf16[4,32,384]{2,1,0:T(8,128)(2,1)S(1)} all-gather(bf16[2,32,384]{2,1,0:T(8,128)(2,1)S(1)} %get-tuple-element.22.cells), channel_id=1, replica_groups={{0,1},{2,3},{4,5},{6,7},{8,9},{10,11},{12,13},{14,15},{16,17},{18,19},{..., dimensions={0}, use_global_device_ids=true | all-gather | bytes 147456 | tf_op jit(solution)/shard_map/all_gather | solution.py:42
  32.4 9.5 %all_gather.27.beside = bf16[8,32,384]{2,1,0:T(8,128)(2,1)S(1)} all-gather(bf16[4,32,384]{2,1,0:T(8,128)(2,1)S(1)} %all_gather.26), channel_id=1, replica_groups={{0,6},{1,511},{2,4},{3,509},{5,11},{7,9},{8,14},{10,12},{13,19},{15,17}..., dimensions={0}, use_global_device_ids=true | all-gather | bytes 294912 | tf_op jit(solution)/shard_map/all_gather | solution.py:69
  42.0 7.3 %all_gather.28.refs_0_ = bf16[24,32,384]{2,1,0:T(8,128)(2,1)S(1)} all-gather(bf16[6,32,384]{2,1,0:T(8,128)(2,1)S(1)} %shard_map.72), channel_id=1, replica_groups=mesh['slab'=128,'col'=4] {'col'}, dimensions={0}, use_global_device_ids=true | all-gather | bytes 737280 | tf_op jit(solution)/shard_map/all_gather | solution.py:101
  49.3 1.5 %shard_map.73 = (f32[2,32,256]{2,1,0:T(8,128)S(1)}, bf16[2,64,384]{2,1,0:T(8,128)(2,1)S(1)}) custom-call(s32[2,6]{1,0:T(2,128)S(1)} %copy-done, f32[2,32,384]{2,1,0:T(8,128)S(1)} %get-tuple-element.14.rhs, bf16[2,256,384]{2,1,0:T(8,128)(2,1)S(1)} %get-tuple-element.15.basis, bf16[2,256,256]{2,1,0:T(8,128)(2,1)S(1)} %get-tuple-element.16.coarse, ...), custom_call_target="tpu_custom_call" | custom-call | tf_op jit(solution)/shard_map/pallas_call | solution.py:294
  50.9 1.9 %all_gather.29 = bf16[4,64,384]{2,1,0:T(8,128)(2,1)S(1)} all-gather(bf16[2,64,384]{2,1,0:T(8,128)(2,1)S(1)} %get-tuple-element.25), channel_id=1, replica_groups={{0,1},{2,3},{4,5},{6,7},{8,9},{10,11},{12,13},{14,15},{16,17},{18,19},{..., dimensions={0}, use_global_device_ids=true | all-gather | bytes 294912 | tf_op jit(solution)/shard_map/all_gather | solution.py:42
  52.8 8.3 %collective-permute-start.1 = (bf16[4,64,384]{2,1,0:T(8,128)(2,1)S(1)}, bf16[4,64,384]{2,1,0:T(8,128)(2,1)S(1)}, u32[]{:S(2)}, u32[]{:S(2)}) collective-permute-start(bf16[4,64,384]{2,1,0:T(8,128)(2,1)S(1)} %all_gather.29), channel_id=1, source_target_pairs={{0,6},{1,511},{2,4},{3,509},{4,2},{5,11},{6,0},{7,9},{8,14},{9,7},... | collective-permute-start | bytes 589832 | tf_op jit(solution)/shard_map/ppermute | solution.py:61
  61.1 5.2 %all_gather.30.refs_0_ = bf16[8,64,384]{2,1,0:T(8,128)(2,1)S(1)} all-gather(bf16[4,64,384]{2,1,0:T(8,128)(2,1)S(1)} %all_gather.29), channel_id=1, replica_groups={{0,2},{1,3},{4,6},{5,7},{8,10},{9,11},{12,14},{13,15},{16,18},{17,19},{..., dimensions={0}, use_global_device_ids=true | all-gather | bytes 589824 | tf_op jit(solution)/shard_map/all_gather | solution.py:42
  66.3 0.0 collective-permute-done.1
  66.3 7.4 %all_gather.31.refs_1_ = bf16[16,64,384]{2,1,0:T(8,128)(2,1)S(1)} all-gather(bf16[4,64,384]{2,1,0:T(8,128)(2,1)S(1)} %collective-permute-done.1), channel_id=1, replica_groups=mesh['slab'=128,'col'=4] {'col'}, dimensions={0}, use_global_device_ids=true | all-gather | bytes 983040 | tf_op jit(solution)/shard_map/all_gather | solution.py:108
  73.6 2.1 %shard_map.74 = (f32[2,32,384]{2,1,0:T(8,128)}, f32[2,32,256]{2,1,0:T(8,128)}) custom-call(s32[2,6]{1,0:T(2,128)S(1)} %copy-done, f32[2,32,256]{2,1,0:T(8,128)S(1)} %get-tuple-element.23.base, f32[2,32,384]{2,1,0:T(8,128)S(1)} %get-tuple-element.24.x_second, bf16[2,256,384]{2,1,0:T(8,128)(2,1)S(1)} %get-tuple-element.15.basis, ...), custom_call_target="tpu_custom_call" | custom-call | tf_op jit(solution)/shard_map/pallas_call | solution.py:300
  (2 shorter events, 0.0 us)
Async XLA Ops:
  0.6 28.6 %copy-start = (s32[2,6]{1,0:T(2,128)S(1)}, s32[2,6]{1,0:T(2,128)}, u32[]{:S(2)}) copy-start(s32[2,6]{1,0:T(2,128)} %nb.5) | copy-start | bytes 148
  10.4 12.6 %collective-permute-start = (bf16[4,32,384]{2,1,0:T(8,128)(2,1)S(1)}, bf16[4,32,384]{2,1,0:T(8,128)(2,1)S(1)}, u32[]{:S(2)}, u32[]{:S(2)}) collective-permute-start(bf16[4,32,384]{2,1,0:T(8,128)(2,1)S(1)} %all_gather.24), channel_id=1, source_target_pairs={{0,6},{1,511},{2,4},{3,509},{4,2},{5,11},{6,0},{7,9},{8,14},{9,7},... | collective-permute-start | bytes 294920 | tf_op jit(solution)/shard_map/ppermute | solution.py:61
  52.8 13.5 %collective-permute-start.1 = (bf16[4,64,384]{2,1,0:T(8,128)(2,1)S(1)}, bf16[4,64,384]{2,1,0:T(8,128)(2,1)S(1)}, u32[]{:S(2)}, u32[]{:S(2)}) collective-permute-start(bf16[4,64,384]{2,1,0:T(8,128)(2,1)S(1)} %all_gather.29), channel_id=1, source_target_pairs={{0,6},{1,511},{2,4},{3,509},{4,2},{5,11},{6,0},{7,9},{8,14},{9,7},... | collective-permute-start | bytes 589832 | tf_op jit(solution)/shard_map/ppermute | solution.py:61

commit v5 on v4

--- a/solution.py
+++ b/solution.py
@@ -290,7 +290,7 @@
         (shape((cells, rows, block), f32), shape((cells, rows, block), bf16)),
         [smem] + [vmem] * (4 + len(near)),
     )(neighbours, rhs, x_first, smoother, tiles, *near)
-    near = joined_exchange(send, slabs, cols, cross_now)
+    near = exchange_apart(send, slabs, cols)
     base, send = call(
         functools.partial(third_body, slab_cells),
         (shape((cells, rows, size), f32), shape((cells, 2 * rows, block), bf16)),

time: 76 us -> 76.1 us (level)
  starting transfers between devices: 18.7 us -> 25 us
  blocking collectives: 47.8 us -> 41.6 us
    all_gather x1 -> x0, blocking collectives: 9.55 us -> none  [cross_now(): lax.all_gather(values, AXES, axis=0, tiled=True, axis_index_groups=pairs(...]
    all_gather x2 -> x1, blocking collectives: 13.5 us -> 6.18 us  [joined_exchange(): return (lax.all_gather(joined, 'col', axis=0, tiled=True),)]
    all_gather x1 -> x2, blocking collectives: 7.37 us -> 13.9 us  [exchange_apart(): return (own, lax.all_gather(beside, 'col', axis=0, tiled=True))]
    ppermute x2 -> x3, starting transfers between devices: 18.7 us -> 25 us  [cross(): lax.ppermute(values, AXES, [(s * cols + c, target(s, c)) for s in range(s...]
    all_gather x4 -> x5, blocking collectives: 17.4 us -> 21.5 us  [gather(): lax.all_gather(values, AXES, axis=0, tiled=True, axis_index_groups=pairs(...]
  transfers between devices with their start and end apart: 2 -> 3, of which waited for: 0 -> 0; matrix products, arithmetic and copies ran while one was open for 0% -> 0% of each run, Pallas kernels for 3% -> 3%
where the time goes in v5:
time: 76.1 us; the launch traced here: 75.8 us
  blocking collectives  41.6 us (55%)
  starting transfers between devices  25 us (33%)
  Pallas kernels  8.52 us (11%)
    ppermute x3, starting transfers between devices, cross(): lax.ppermute(values, AXES, [(s * cols + c, target(s, c)) for s in range(s...  25 us
    all_gather x5, blocking collectives, gather(): lax.all_gather(values, AXES, axis=0, tiled=True, axis_index_groups=pairs(...  21.5 us
    all_gather x2, blocking collectives, exchange_apart(): return (own, lax.all_gather(beside, 'col', axis=0, tiled=True))  13.9 us
    all_gather x1, blocking collectives, joined_exchange(): return (lax.all_gather(joined, 'col', axis=0, tiled=True),)  6.18 us
    pallas_call x1, Pallas kernels, per_device(): call(coarse_body, (shape(tiles.shape, bf16), shape(basis.shape, bf16), sh...  2.18 us
    pallas_call x1, Pallas kernels, per_device(): call(functools.partial(fourth_body, slab_cells), (shape((cells, rows, blo...  2.08 us
  transfers between devices with their start and end apart: 3, of which 0 were waited for; matrix products, arithmetic and copies ran while one was open for 0% of the time, Pallas kernels for 3%

profile of v5, /device:TPU:1, one launch (start us, length us, event | category | flops | bytes accessed | tf_op | source)
XLA Modules:
  0.0 75.8 jit_solution(2211103979335560514)
XLA Ops:
  0.6 0.0 copy-start
  0.6 1.4 %shard_map.68 = (f32[2,32,384]{2,1,0:T(8,128)S(1)}, bf16[2,32,384]{2,1,0:T(8,128)(2,1)S(1)}, bf16[2,384,384]{2,1,0:T(8,128)(2,1)S(1)}, f32[2,32,384]{2,1,0:T(8,128)S(1)}) custom-call(bf16[2,384,384]{2,1,0:T(8,128)(2,1)} %smoother_hbm.1, f32[2,32,384]{2,1,0:T(8,128)} %rhs_hbm.1), custom_call_target="tpu_custom_call" | custom-call | tf_op jit(solution)/shard_map/pallas_call | solution.py:265
  2.0 8.4 %all_gather.24 = bf16[4,32,384]{2,1,0:T(8,128)(2,1)S(1)} all-gather(bf16[2,32,384]{2,1,0:T(8,128)(2,1)S(1)} %get-tuple-element.21.cells), channel_id=1, replica_groups={{0,1},{2,3},{4,5},{6,7},{8,9},{10,11},{12,13},{14,15},{16,17},{18,19},{..., dimensions={0}, use_global_device_ids=true | all-gather | bytes 147456 | tf_op jit(solution)/shard_map/all_gather | solution.py:42
  10.4 10.4 %collective-permute-start = (bf16[4,32,384]{2,1,0:T(8,128)(2,1)S(1)}, bf16[4,32,384]{2,1,0:T(8,128)(2,1)S(1)}, u32[]{:S(2)}, u32[]{:S(2)}) collective-permute-start(bf16[4,32,384]{2,1,0:T(8,128)(2,1)S(1)} %all_gather.24), channel_id=1, source_target_pairs={{0,6},{1,511},{2,4},{3,509},{4,2},{5,11},{6,0},{7,9},{8,14},{9,7},... | collective-permute-start | bytes 294920 | tf_op jit(solution)/shard_map/ppermute | solution.py:61
  20.8 2.2 %shard_map.69 = (bf16[2,6,384,384]{3,2,1,0:T(8,128)(2,1)S(1)}, bf16[2,256,384]{2,1,0:T(8,128)(2,1)S(1)}, bf16[2,256,256]{2,1,0:T(8,128)(2,1)S(1)}, f32[2,1,256]{2,1,0:T(1,128)S(1)}) custom-call(bf16[2,6,384,384]{3,2,1,0:T(8,128)(2,1)} %tiles_hbm.1, bf16[2,256,384]{2,1,0:T(8,128)(2,1)} %basis_hbm.1), custom_call_target="tpu_custom_call" | custom-call | tf_op jit(solution)/shard_map/pallas_call | solution.py:276
  23.0 0.0 collective-permute-done.beside
  23.0 6.2 %all_gather.25.refs_0_ = bf16[24,32,384]{2,1,0:T(8,128)(2,1)S(1)} all-gather(bf16[6,32,384]{2,1,0:T(8,128)(2,1)S(1)} %shard_map.70), channel_id=1, replica_groups=mesh['slab'=128,'col'=4] {'col'}, dimensions={0}, use_global_device_ids=true | all-gather | bytes 737280 | tf_op jit(solution)/shard_map/all_gather | solution.py:101
  29.2 0.0 copy-done
  29.2 1.4 %shard_map.71 = (f32[2,32,384]{2,1,0:T(8,128)S(1)}, bf16[2,32,384]{2,1,0:T(8,128)(2,1)S(1)}) custom-call(s32[2,6]{1,0:T(2,128)S(1)} %copy-done, f32[2,32,384]{2,1,0:T(8,128)S(1)} %get-tuple-element.14.rhs, f32[2,32,384]{2,1,0:T(8,128)S(1)} %get-tuple-element.19.x_first, bf16[2,384,384]{2,1,0:T(8,128)(2,1)S(1)} %get-tuple-element.20.smoother, ...), custom_call_target="tpu_custom_call" | custom-call | tf_op jit(solution)/shard_map/pallas_call | solution.py:288
  30.6 1.9 %all_gather.26 = bf16[4,32,384]{2,1,0:T(8,128)(2,1)S(1)} all-gather(bf16[2,32,384]{2,1,0:T(8,128)(2,1)S(1)} %get-tuple-element.22), channel_id=1, replica_groups={{0,1},{2,3},{4,5},{6,7},{8,9},{10,11},{12,13},{14,15},{16,17},{18,19},{..., dimensions={0}, use_global_device_ids=true | all-gather | bytes 147456 | tf_op jit(solution)/shard_map/all_gather | solution.py:42
  32.4 8.0 %collective-permute-start.1 = (bf16[4,32,384]{2,1,0:T(8,128)(2,1)S(1)}, bf16[4,32,384]{2,1,0:T(8,128)(2,1)S(1)}, u32[]{:S(2)}, u32[]{:S(2)}) collective-permute-start(bf16[4,32,384]{2,1,0:T(8,128)(2,1)S(1)} %all_gather.26), channel_id=1, source_target_pairs={{0,6},{1,511},{2,4},{3,509},{4,2},{5,11},{6,0},{7,9},{8,14},{9,7},... | collective-permute-start | bytes 294920 | tf_op jit(solution)/shard_map/ppermute | solution.py:61
  40.4 4.1 %all_gather.27.refs_0_ = bf16[8,32,384]{2,1,0:T(8,128)(2,1)S(1)} all-gather(bf16[4,32,384]{2,1,0:T(8,128)(2,1)S(1)} %all_gather.26), channel_id=1, replica_groups={{0,2},{1,3},{4,6},{5,7},{8,10},{9,11},{12,14},{13,15},{16,18},{17,19},{..., dimensions={0}, use_global_device_ids=true | all-gather | bytes 294912 | tf_op jit(solution)/shard_map/all_gather | solution.py:42
  44.5 0.0 collective-permute-done.1
  44.5 6.6 %all_gather.28.refs_1_ = bf16[16,32,384]{2,1,0:T(8,128)(2,1)S(1)} all-gather(bf16[4,32,384]{2,1,0:T(8,128)(2,1)S(1)} %collective-permute-done.1), channel_id=1, replica_groups=mesh['slab'=128,'col'=4] {'col'}, dimensions={0}, use_global_device_ids=true | all-gather | bytes 491520 | tf_op jit(solution)/shard_map/all_gather | solution.py:108
  51.1 1.5 %shard_map.72 = (f32[2,32,256]{2,1,0:T(8,128)S(1)}, bf16[2,64,384]{2,1,0:T(8,128)(2,1)S(1)}) custom-call(s32[2,6]{1,0:T(2,128)S(1)} %copy-done, f32[2,32,384]{2,1,0:T(8,128)S(1)} %get-tuple-element.14.rhs, bf16[2,256,384]{2,1,0:T(8,128)(2,1)S(1)} %get-tuple-element.15.basis, bf16[2,256,256]{2,1,0:T(8,128)(2,1)S(1)} %get-tuple-element.16.coarse, ...), custom_call_target="tpu_custom_call" | custom-call | tf_op jit(solution)/shard_map/pallas_call | solution.py:294
  52.6 1.9 %all_gather.29 = bf16[4,64,384]{2,1,0:T(8,128)(2,1)S(1)} all-gather(bf16[2,64,384]{2,1,0:T(8,128)(2,1)S(1)} %get-tuple-element.25), channel_id=1, replica_groups={{0,1},{2,3},{4,5},{6,7},{8,9},{10,11},{12,13},{14,15},{16,17},{18,19},{..., dimensions={0}, use_global_device_ids=true | all-gather | bytes 294912 | tf_op jit(solution)/shard_map/all_gather | solution.py:42
  54.6 6.6 %collective-permute-start.2 = (bf16[4,64,384]{2,1,0:T(8,128)(2,1)S(1)}, bf16[4,64,384]{2,1,0:T(8,128)(2,1)S(1)}, u32[]{:S(2)}, u32[]{:S(2)}) collective-permute-start(bf16[4,64,384]{2,1,0:T(8,128)(2,1)S(1)} %all_gather.29), channel_id=1, source_target_pairs={{0,6},{1,511},{2,4},{3,509},{4,2},{5,11},{6,0},{7,9},{8,14},{9,7},... | collective-permute-start | bytes 589832 | tf_op jit(solution)/shard_map/ppermute | solution.py:61
  61.2 5.2 %all_gather.30.refs_0_ = bf16[8,64,384]{2,1,0:T(8,128)(2,1)S(1)} all-gather(bf16[4,64,384]{2,1,0:T(8,128)(2,1)S(1)} %all_gather.29), channel_id=1, replica_groups={{0,2},{1,3},{4,6},{5,7},{8,10},{9,11},{12,14},{13,15},{16,18},{17,19},{..., dimensions={0}, use_global_device_ids=true | all-gather | bytes 589824 | tf_op jit(solution)/shard_map/all_gather | solution.py:42
  66.4 0.0 collective-permute-done.2
  66.4 7.3 %all_gather.31.refs_1_ = bf16[16,64,384]{2,1,0:T(8,128)(2,1)S(1)} all-gather(bf16[4,64,384]{2,1,0:T(8,128)(2,1)S(1)} %collective-permute-done.2), channel_id=1, replica_groups=mesh['slab'=128,'col'=4] {'col'}, dimensions={0}, use_global_device_ids=true | all-gather | bytes 983040 | tf_op jit(solution)/shard_map/all_gather | solution.py:108
  73.8 2.1 %shard_map.73 = (f32[2,32,384]{2,1,0:T(8,128)}, f32[2,32,256]{2,1,0:T(8,128)}) custom-call(s32[2,6]{1,0:T(2,128)S(1)} %copy-done, f32[2,32,256]{2,1,0:T(8,128)S(1)} %get-tuple-element.23.base, f32[2,32,384]{2,1,0:T(8,128)S(1)} %get-tuple-element.24.x_second, bf16[2,256,384]{2,1,0:T(8,128)(2,1)S(1)} %get-tuple-element.15.basis, ...), custom_call_target="tpu_custom_call" | custom-call | tf_op jit(solution)/shard_map/pallas_call | solution.py:300
  (1 shorter events, 0.0 us)
Async XLA Ops:
  0.6 28.6 %copy-start = (s32[2,6]{1,0:T(2,128)S(1)}, s32[2,6]{1,0:T(2,128)}, u32[]{:S(2)}) copy-start(s32[2,6]{1,0:T(2,128)} %nb.5) | copy-start | bytes 148
  10.4 12.6 %collective-permute-start = (bf16[4,32,384]{2,1,0:T(8,128)(2,1)S(1)}, bf16[4,32,384]{2,1,0:T(8,128)(2,1)S(1)}, u32[]{:S(2)}, u32[]{:S(2)}) collective-permute-start(bf16[4,32,384]{2,1,0:T(8,128)(2,1)S(1)} %all_gather.24), channel_id=1, source_target_pairs={{0,6},{1,511},{2,4},{3,509},{4,2},{5,11},{6,0},{7,9},{8,14},{9,7},... | collective-permute-start | bytes 294920 | tf_op jit(solution)/shard_map/ppermute | solution.py:61
  32.4 12.1 %collective-permute-start.1 = (bf16[4,32,384]{2,1,0:T(8,128)(2,1)S(1)}, bf16[4,32,384]{2,1,0:T(8,128)(2,1)S(1)}, u32[]{:S(2)}, u32[]{:S(2)}) collective-permute-start(bf16[4,32,384]{2,1,0:T(8,128)(2,1)S(1)} %all_gather.26), channel_id=1, source_target_pairs={{0,6},{1,511},{2,4},{3,509},{4,2},{5,11},{6,0},{7,9},{8,14},{9,7},... | collective-permute-start | bytes 294920 | tf_op jit(solution)/shard_map/ppermute | solution.py:61
  54.6 11.8 %collective-permute-start.2 = (bf16[4,64,384]{2,1,0:T(8,128)(2,1)S(1)}, bf16[4,64,384]{2,1,0:T(8,128)(2,1)S(1)}, u32[]{:S(2)}, u32[]{:S(2)}) collective-permute-start(bf16[4,64,384]{2,1,0:T(8,128)(2,1)S(1)} %all_gather.29), channel_id=1, source_target_pairs={{0,6},{1,511},{2,4},{3,509},{4,2},{5,11},{6,0},{7,9},{8,14},{9,7},... | collective-permute-start | bytes 589832 | tf_op jit(solution)/shard_map/ppermute | solution.py:61
